TPU v7x, 32 devices: a whole 2x2x4 slice. The times are simulated.
32 devices in a mesh: seq: 8 (over z, y), batch: 4 (over x, core).
Axes of the slice: x: 2, y: 2, z: 4, core: 2. Of those that a mesh axis runs over, the one named last changes fastest.
Arguments:
- inputs: bfloat16 [8, 2048, 768], P('batch', 'seq'), may hold values from -6 to 6
- lengths: int32 [8], P('batch'), may hold values from 512 to 2048, as said below
- cotangent: bfloat16 [8, 2048, 768], P('batch', 'seq'), may hold values from -6 to 6
- local_query: bfloat16 [768, 768], replicated, may hold values from -0.21875 to 0.21875
- local_query_bias: float32 [768], replicated, may hold values from -3 to 3
- local_key: bfloat16 [768, 768], replicated, may hold values from -0.21875 to 0.21875
- local_value: bfloat16 [768, 768], replicated, may hold values from -0.21875 to 0.21875
- local_value_bias: float32 [768], replicated, may hold values from -3 to 3
- local_output: bfloat16 [768, 768], replicated, may hold values from -0.875 to 0.875
- local_output_bias: float32 [768], replicated, may hold values from -3 to 3
- pooled_query: bfloat16 [768, 768], replicated, may hold values from -0.15625 to 0.15625
- pooled_query_bias: float32 [768], replicated, may hold values from -3 to 3
- pooled_output: bfloat16 [768, 768], replicated, may hold values from -1.25 to 1.25
- pooled_output_bias: float32 [768], replicated, may hold values from -3 to 3
- conv_key: float32 [768, 5], replicated, may hold values from -2.5 to 2.5
- conv_value: float32 [768, 5], replicated, may hold values from -2.5 to 2.5
- conv_value_bias: float32 [768], replicated, may hold values from -3 to 3
- norm_gain: float32 [768], replicated, may hold values from 0.5 to 1.5
- norm_shift: float32 [768], replicated, may hold values from -1.75 to 1.75
- expand_weight: bfloat16 [768, 3072], replicated, may hold values from -0.21875 to 0.21875
- expand_bias: float32 [3072], replicated, may hold values from -3 to 3
- reduce_weight: bfloat16 [3072, 768], replicated, may hold values from -0.109375 to 0.109375
- reduce_bias: float32 [768], replicated, may hold values from -3 to 3
- final_gain: float32 [768], replicated, may hold values from 0.5 to 1.5
- final_shift: float32 [768], replicated, may hold values from -1.75 to 1.75
Outputs:
- outputs: bfloat16 [8, 2048, 768], P('batch', 'seq')
- input_grad: bfloat16 [8, 2048, 768], P('batch', 'seq')
- grad_local_query: float32 [768, 768], P('seq')
- grad_local_query_bias: float32 [768], P('seq')
- grad_local_key: float32 [768, 768], P('seq')
- grad_local_value: float32 [768, 768], P('seq')
- grad_local_value_bias: float32 [768], P('seq')
- grad_local_output: float32 [768, 768], P('seq')
- grad_local_output_bias: float32 [768], P('seq')
- grad_pooled_query: float32 [768, 768], P('seq')
- grad_pooled_query_bias: float32 [768], P('seq')
- grad_pooled_output: float32 [768, 768], P('seq')
- grad_pooled_output_bias: float32 [768], P('seq')
- grad_conv_key: float32 [768, 5], P('seq')
- grad_conv_value: float32 [768, 5], P('seq')
- grad_conv_value_bias: float32 [768], P('seq')
- grad_norm_gain: float32 [768], P('seq')
- grad_norm_shift: float32 [768], P('seq')
- grad_expand_weight: float32 [768, 3072], P('seq')
- grad_expand_bias: float32 [3072], P('seq')
- grad_reduce_weight: float32 [3072, 768], P('seq')
- grad_reduce_bias: float32 [768], P('seq')
- grad_final_gain: float32 [768], P('seq')
- grad_final_shift: float32 [768], P('seq')
Inputs may be any that keep to these rules, and one draw needn't show every extreme that they name: `lengths`: each document fills its slots from the first one and is padded at its end; documents b with the same b // 2 form a group, and in each group one document, drawn from the seed, fills all 2048 slots.
All inputs are finite; a program needn't handle non-finite values.
Results may differ from a plain program's by a relative error of at most 0.029.
The roundings to bfloat16 on the way count: a program that leaves them out, or rounds other values in their place, can miss the bound.
Values may be sent and summed in bfloat16 or wider, within the bound.
No kernel may reach another device: no remote copies, remote signals or barrier semaphores. Data moves between devices by JAX's collectives and lax.ppermute only.
A program may use at most 192 MiB of HBM per device.

v0:
```python
import functools
import math

import jax
import jax.numpy as jnp
from jax import lax
from jax.experimental import pallas as pl
from jax.experimental.pallas import tpu as pltpu
from jax.sharding import PartitionSpec as P

HEADS = 12
HD = 64
WIN = 128
PWIN = 512
KER = 5
STRIDE = 4
HALF = WIN // 2
REACH = PWIN // 2
NEGATIVE = -1e30
SCALE = 1.0 / math.sqrt(HD)
EPSILON = 1e-05
LANES = 128
TILE = 128
ROWS = 128
CHUNK = 768
PAIRS = 2
F32 = jnp.float32
BF16 = jnp.bfloat16


def nn(left, right):
    return jnp.dot(left, right, preferred_element_type=F32)


def nt(left, right):
    return lax.dot_general(left, right, (((1,), (1,)), ((), ())), preferred_element_type=F32)


def tn(left, right):
    return lax.dot_general(left, right, (((0,), (0,)), ((), ())), preferred_element_type=F32)


def column_sum(block):
    return jnp.sum(block.astype(F32), axis=0, keepdims=True)


def call(body, grid, scalars, inputs, outputs, scratch=(), spare=8):
    used = spare * 2**20
    arrays, in_specs, out_specs, shapes = [], [], [], []

    def spec(shape, dtype, block, index):
        nonlocal used
        if block is None:
            return pl.BlockSpec(memory_space=pltpu.VMEM)
        if block == "raw":
            return pl.BlockSpec(memory_space=pl.ANY)
        used += 2 * math.prod(block) * jnp.dtype(dtype).itemsize
        return pl.BlockSpec(block, index)

    for array, block, index in inputs:
        in_specs.append(spec(array.shape, array.dtype, block, index))
        if block is not None:
            array = pltpu.with_memory_space_constraint(array, pltpu.HBM)
        arrays.append(array)
    for shape, dtype, block, index in outputs:
        out_specs.append(spec(shape, dtype, block, index))
        plain = block is None
        shapes.append((jax.ShapeDtypeStruct if plain else pltpu.HBM)(shape, dtype))
    for item in scratch:
        if hasattr(item, "shape") and item.memory_space == pltpu.VMEM:
            used += math.prod(item.shape) * jnp.dtype(item.dtype).itemsize
    return pl.pallas_call(
        body,
        grid_spec=pltpu.PrefetchScalarGridSpec(
            num_scalar_prefetch=len(scalars),
            grid=grid,
            in_specs=in_specs,
            out_specs=out_specs,
            scratch_shapes=list(scratch),
        ),
        out_shape=shapes,
        compiler_params=pltpu.CompilerParams(
            dimension_semantics=("arbitrary",) * len(grid), vmem_limit_bytes=used
        ),
        cost_estimate=pl.CostEstimate(flops=1000, bytes_accessed=1000, transcendentals=0),
    )(*scalars, *arrays)


def raw(array):
    return (array, "raw", None)


def out_raw(shape, dtype):
    return (shape, dtype, "raw", None)


def whole(array):
    return (array, None, None)


def out_whole(shape, dtype):
    return (shape, dtype, None, None)


def sync(*values):
    return lax.optimization_barrier(values)


def stack_heads(block):
    lane = lax.broadcasted_iota(jnp.int32, block.shape, 1)
    zero = jnp.zeros_like(block)
    return jnp.concatenate(
        [jnp.where(lane < HD, block, zero), jnp.where(lane < HD, zero, block)], axis=0
    )


def unstack(block):
    half = block.shape[1] // 2
    joined = jnp.concatenate([block[:HD, :half], block[HD:, half:]], axis=0)
    return joined.T


def positions(shape, dim):
    return lax.broadcasted_iota(jnp.int32, shape, dim)


def project_body(place, x_far, wq_far, bq, wk_far, wv_far, bv, q, k, v, wk, wv, x, wq, sems):
    docs, rows, width = x.shape
    fetches = [
        pltpu.make_async_copy(far, near, sems.at[index])
        for index, (far, near) in enumerate(
            ((x_far, x), (wq_far, wq), (wk_far, wk), (wv_far, wv))
        )
    ]
    for fetch in fetches:
        fetch.start()
    fetches[0].wait()
    flat = x[...].reshape(docs * rows, width)
    fetches[1].wait()
    q[...] = (nn(flat, wq[...]) + bq[...]).astype(BF16).reshape(q.shape)
    fetches[2].wait()
    k[...] = nn(flat, wk[...]).astype(BF16).reshape(k.shape)
    fetches[3].wait()
    v[...] = (nn(flat, wv[...]) + bv[...]).astype(BF16).reshape(v.shape)


def project(place, x, wq, bq, wk, wv, bv):
    return call(
        project_body,
        (1,),
        (place,),
        [raw(x), raw(wq), whole(bq), raw(wk), raw(wv), whole(bv)],
        [out_whole(x.shape, BF16)] * 3 + [out_whole(wk.shape, BF16)] * 2,
        [
            pltpu.VMEM(x.shape, BF16),
            pltpu.VMEM(wq.shape, BF16),
            pltpu.SemaphoreType.DMA((4,)),
        ],
    )


def pool_body(place, left, right, k, v, wk, wv, bv, ck, cv, bcv, kx, vx, pooled, rows):
    offset = place[0]
    docs, own_rows, width = k.shape
    rims = jnp.concatenate(
        [part[doc] for doc in range(docs) for part in (left, right)], axis=0
    )
    size = own_rows + WIN
    count = pooled.shape[2]
    spot = offset - HALF + positions((size, 1), 0)
    for which, (weight, bias, taps, own, out) in enumerate(
        ((wk, None, ck, k, kx), (wv, bv, cv, v, vx))
    ):
        value = nn(rims, weight[...])
        if bias is not None:
            value = value + bias[...]
        value = value.astype(BF16)
        for doc in range(docs):
            at = doc * WIN
            out[doc, :HALF] = value[at : at + HALF]
            out[doc, HALF : HALF + own_rows] = own[doc]
            out[doc, HALF + own_rows :] = value[at + HALF : at + WIN]
            valid = (spot >= 0) & (spot < place[1 + doc])
            for group in range(width // LANES):
                lanes = slice(group * LANES, (group + 1) * LANES)
                rows[group] = jnp.where(valid, out[doc, :, lanes].astype(F32), 0.0)
                total = jnp.zeros((count, LANES), F32)
                for tap in range(KER):
                    start = HALF - KER // 2 + tap
                    read = rows[group, pl.ds(start, count, stride=STRIDE), :]
                    total = total + read * taps[tap : tap + 1, lanes]
                if which == 1:
                    total = total + bcv[:, lanes]
                pooled[which, doc, :, lanes] = total.astype(BF16)


def pool(place, left, right, k, v, wk, wv, bv, ck, cv, bcv):
    docs, rows, width = k.shape
    extended = rows + WIN
    return call(
        pool_body,
        (1,),
        (place,),
        [whole(a) for a in (left, right, k, v, wk, wv, bv, ck, cv, bcv)],
        [
            out_whole((docs, extended, width), BF16),
            out_whole((docs, extended, width), BF16),
            out_whole((2, docs, rows // STRIDE, width), BF16),
        ],
        [pltpu.VMEM((width // LANES, extended, LANES), F32)],
    )


def local_bias(tile, offset, length):
    shape = (TILE + WIN, TILE)
    key = positions(shape, 0)
    query = positions(shape, 1)
    spot = offset + tile * TILE - HALF + key
    allowed = (
        (key >= query) & (key < query + WIN) & (spot >= 0) & (spot < length)
    ) | (key == query + HALF)
    return jnp.where(allowed, 0.0, NEGATIVE)


def softmax_columns(scores):
    top = jnp.max(scores, axis=0, keepdims=True)
    grown = jnp.exp(scores - top)
    return grown * (1.0 / jnp.sum(grown, axis=0, keepdims=True))


def local_forward_body(place, q, kx, vx, mix, probs, *, doc):
    offset, length = place[0], place[1 + doc]
    span = TILE + WIN
    for tile in range(q.shape[1] // TILE):
        half_bias = local_bias(tile, offset, length)
        bias = jnp.concatenate([half_bias, half_bias], axis=1)
        first = tile * TILE
        for pair in range(q.shape[2] // LANES):
            lanes = slice(pair * LANES, (pair + 1) * LANES)
            queries = stack_heads(q[doc, first : first + TILE, lanes]) * SCALE
            scores = nt(kx[doc, first : first + span, lanes], queries) + bias
            chance = softmax_columns(scores)
            probs[pair, tile] = chance
            turned = vx[doc, first : first + span, lanes].T
            mixed = nn(turned, chance.astype(BF16))
            mix[first : first + TILE, lanes] = unstack(mixed).astype(BF16)


def local_forward(place, q, kx, vx, doc):
    _, rows, width = q.shape
    pairs, tiles, span = width // LANES, rows // TILE, TILE + WIN
    return call(
        functools.partial(local_forward_body, doc=doc),
        (1,),
        (place,),
        [whole(a) for a in (q, kx, vx)],
        [
            out_whole((rows, width), BF16),
            out_whole((pairs, tiles, span, 2 * TILE), F32),
        ],
    )


def middle_body(place, x, wo, bo, wpq, bpq, *refs):
    docs, rows = x.shape[0], x.shape[1]
    mixes, (mix, middle, middle_low, q2) = refs[:docs], refs[docs:]
    for doc in range(docs):
        mix[doc] = mixes[doc][...]
    flat = docs * rows
    branch = nn(mix[...].reshape(flat, x.shape[2]), wo[...]) + bo[...]
    total = x[...].reshape(flat, x.shape[2]).astype(F32) + branch
    middle[...] = total.reshape(middle.shape)
    low = total.astype(BF16)
    middle_low[...] = low.reshape(middle_low.shape)
    q2[...] = (nn(low, wpq[...]) + bpq[...]).astype(BF16).reshape(q2.shape)


def middle_forward(place, x, wo, bo, wpq, bpq, mixes):
    docs, rows, width = x.shape
    return call(
        middle_body,
        (1,),
        (place,),
        [whole(a) for a in (x, wo, bo, wpq, bpq, *mixes)],
        [
            out_whole((docs, rows, width), BF16),
            out_whole((docs, rows, width), F32),
            out_whole((docs, rows, width), BF16),
            out_whole((docs, rows, width), BF16),
        ],
    )


def attention_back(keys, values, queries, grads, chance):
    stacked_grads = stack_heads(grads)
    stacked_queries = stack_heads(queries)
    grad_chance = nt(values, stacked_grads * SCALE)
    dots = jnp.sum(chance * grad_chance, axis=0, keepdims=True)
    grad_raw = (chance * (grad_chance - dots)).astype(BF16)
    grad_keys = nn(grad_raw, stacked_queries)
    grad_values = nn(chance.astype(BF16), stacked_grads)
    grad_queries = unstack(nn(keys.T, grad_raw))
    return grad_queries, grad_keys, grad_values


def first_back_body(place, gq2, gsum, wpq, wo, gmid, gfirst, gmix, vec):
    docs, rows, width = gsum.shape
    flat = docs * rows
    grads = gq2[...].reshape(flat, width)
    total = gsum[...].reshape(flat, width) + nt(grads, wpq[...])
    gmid[...] = total.reshape(gmid.shape)
    low = total.astype(BF16)
    gfirst[...] = low
    gmix[...] = nt(low, wo[...]).astype(BF16).reshape(gmix.shape)
    vec[...] = jnp.zeros_like(vec)
    vec[0:1] = column_sum(grads)
    vec[1:2] = column_sum(low)


def first_backward(place, gq2, gsum, wpq, wo):
    docs, rows, width = gsum.shape
    return call(
        first_back_body,
        (1,),
        (place,),
        [whole(a) for a in (gq2, gsum, wpq, wo)],
        [
            out_whole((docs, rows, width), F32),
            out_whole((docs * rows, width), BF16),
            out_whole((docs, rows, width), BF16),
            out_whole((8, width), F32),
        ],
    )


def local_backward_body(place, q, kx, vx, gmix, probs, *refs, doc):
    earlier = refs[: len(refs) - 6]
    dq, own, low_left, low_right, dk, dv = refs[len(refs) - 6 :]
    rows = q.shape[1]
    for old, new in zip(earlier, (dq, own, low_left, low_right)):
        new[:doc] = old[...]
    span = TILE + WIN
    dk[...] = jnp.zeros_like(dk)
    dv[...] = jnp.zeros_like(dv)
    for tile in range(rows // TILE):
        first = tile * TILE
        for pair in range(q.shape[2] // LANES):
            lanes = slice(pair * LANES, (pair + 1) * LANES)
            grad_q, grad_k, grad_v = attention_back(
                kx[doc, first : first + span, lanes],
                vx[doc, first : first + span, lanes],
                q[doc, first : first + TILE, lanes],
                gmix[doc, first : first + TILE, lanes],
                probs[pair, tile],
            )
            dq[doc, first : first + TILE, lanes] = grad_q.astype(BF16)
            dk[first : first + span, lanes] += grad_k
            dv[first : first + span, lanes] += grad_v
    for which, part in enumerate((dk, dv)):
        own[doc, which] = part[HALF : HALF + rows]
        low_left[doc, which] = part[:HALF].astype(BF16)
        low_right[doc, which] = part[HALF + rows :].astype(BF16)


def local_backward(place, q, kx, vx, gmix, probs, doc, earlier=()):
    _, rows, width = q.shape
    span = TILE + WIN
    return call(
        functools.partial(local_backward_body, doc=doc),
        (1,),
        (place,),
        [whole(a) for a in (q, kx, vx, gmix, probs, *earlier)],
        [
            out_whole((doc + 1, rows, width), BF16),
            out_whole((doc + 1, 2, rows, width), F32),
            out_whole((doc + 1, 2, HALF, width), BF16),
            out_whole((doc + 1, 2, HALF, width), BF16),
        ],
        [
            pltpu.VMEM((rows + WIN, width), F32),
            pltpu.VMEM((rows + WIN, width), F32),
        ],
    )


def pooled_forward_body(place, slots, *refs, pieces):
    key_pieces = refs[:pieces]
    value_pieces = refs[pieces : 2 * pieces]
    (
        q2, middle, wpo, bpo, we, wr,
        keys_out, values_out, probs, mix, summed, we_near, wr_near,
        keys, values, bias, sems,
    ) = refs[2 * pieces :]
    doc, pair = pl.program_id(0), pl.program_id(1)
    fetches = [
        pltpu.make_async_copy(we, we_near, sems.at[0]),
        pltpu.make_async_copy(wr, wr_near, sems.at[1]),
    ]
    last = (pair == pl.num_programs(1) - 1) & (doc == pl.num_programs(0) - 1)
    leaves = [
        pltpu.make_async_copy(keys.at[each], keys_out.at[each], sems.at[2 + each])
        for each in range(keys.shape[0])
    ] + [
        pltpu.make_async_copy(
            values.at[each], values_out.at[each], sems.at[2 + keys.shape[0] + each]
        )
        for each in range(keys.shape[0])
    ]

    @pl.when((pair == 0) & (doc == 0))
    def _():
        for fetch in fetches:
            fetch.start()

    offset, length, base = place[0], place[1 + doc], place[1 + pl.num_programs(0)]
    count = keys.shape[1]

    @pl.when(pair == 0)
    def _():
        for where, group, out in ((0, key_pieces, keys), (1, value_pieces, values)):
            at = 0
            for piece in group:
                size = piece.shape[2]
                for block in range(piece.shape[0]):
                    spot = pl.multiple_of(slots[where, at] * size, size)
                    out[doc, pl.ds(spot, size), :] = piece[block, doc]
                    at += 1
        if True:
            shape = (count, q2.shape[1])
            spot = base + positions(shape, 0)
            centre = offset // STRIDE + positions(shape, 1) // STRIDE
            allowed = (
                (spot >= centre - REACH)
                & (spot < centre + REACH)
                & (spot >= 0)
                & (spot * STRIDE < length)
            ) | (spot == centre)
            bias[...] = jnp.where(allowed, 0.0, NEGATIVE)
        for each in range(keys.shape[0]):

            @pl.when(doc == each)
            def _():
                leaves[each].start()
                leaves[keys.shape[0] + each].start()

    for each in range(PAIRS):
        lanes = pl.ds(pl.multiple_of((pair * PAIRS + each) * LANES, LANES), LANES)
        queries = stack_heads(q2[doc, :, lanes]) * SCALE
        half_bias = bias[...]
        scores = nt(keys[doc, :, lanes], queries) + jnp.concatenate([half_bias, half_bias], axis=1)
        chance = softmax_columns(scores)
        probs[0, each] = chance
        mixed = nn(values[doc, :, lanes].T, chance.astype(BF16))
        mix[doc, :, lanes] = unstack(mixed).astype(BF16)

    @pl.when(last)
    def _():
        for copy in fetches + leaves:
            copy.wait()
        flat = (mix.shape[0] * mix.shape[1], mix.shape[2])
        second = nn(mix[...].reshape(flat), wpo[...]) + bpo[...]
        summed[...] = middle[...] + second.reshape(summed.shape)


def pooled_forward(place, slots, key_pieces, value_pieces, q2, middle, wpo, bpo, we, wr):
    docs, rows, width = q2.shape
    pairs, tiles = width // LANES, rows // TILE
    size = key_pieces[0].shape[2]
    count = size * slots.shape[1]

    return call(
        functools.partial(pooled_forward_body, pieces=len(key_pieces)),
        (docs, pairs // PAIRS),
        (place, slots),
        [whole(a) for a in (*key_pieces, *value_pieces, q2, middle, wpo, bpo)]
        + [raw(we), raw(wr)],
        [
            out_raw((docs, count, width), BF16),
            out_raw((docs, count, width), BF16),
            (
                (docs, pairs, count, 2 * rows),
                F32,
                (1, PAIRS, count, 2 * rows),
                lambda doc, pair, *_: (doc, pair, 0, 0),
            ),
            out_whole((docs, rows, width), BF16),
            out_whole((docs, rows, width), F32),
            out_whole(we.shape, BF16),
            out_whole(wr.shape, BF16),
        ],
        [
            pltpu.VMEM((docs, count, width), BF16),
            pltpu.VMEM((docs, count, width), BF16),
            pltpu.VMEM((count, rows), F32),
            pltpu.SemaphoreType.DMA((2 + 2 * docs,)),
        ],
    )


def pooled_backward_body(
    places, token, q2, keys, values, probs, grads, dq, dk_kept, dk_sent, dv_kept, dv_sent, sums
):
    doc, step = pl.program_id(0), pl.program_id(1)
    size = dk_kept.shape[2]
    half = dk_kept.shape[0]
    rows = keys.shape[1]
    for each in range(PAIRS):
        inner = slice(each * LANES, (each + 1) * LANES)
        lanes = pl.ds(pl.multiple_of((step * PAIRS + each) * LANES, LANES), LANES)
        grad_q, *total = attention_back(
            keys[0, :, inner], values[0, :, inner], q2[0, :, inner], grads[0, :, inner],
            probs[0, each],
        )
        dq[doc, :, lanes] = grad_q.astype(BF16)
        for which, (kept, sent) in enumerate(((dk_kept, dk_sent), (dv_kept, dv_sent))):
            sums[each, which, :rows] = total[which]
            sums[each, which, rows:] = jnp.zeros((8, LANES), F32)
            for block in range(half + sent.shape[0]):
                start = pl.multiple_of(places[which, block] * (size - 8), size - 8)
                part = sums[each, which, pl.ds(start, size), :]
                if block < half:
                    kept[block, doc, :, lanes] = part
                else:
                    sent[block - half, doc, :, lanes] = part.astype(BF16)


def pooled_backward(places, token, q2, keys, values, probs, grads, size, kept):
    docs, rows, width = q2.shape
    count = keys.shape[1]
    blocks = count // size
    tiles = rows // TILE

    def lanes_of(array):
        return (array, (1, array.shape[1], PAIRS * LANES), lambda doc, pair, *_: (doc, 0, pair))

    return call(
        pooled_backward_body,
        (docs, width // LANES // PAIRS),
        (places, token),
        [
            lanes_of(q2),
            lanes_of(keys),
            lanes_of(values),
            (
                probs,
                (1, PAIRS, count, 2 * rows),
                lambda doc, pair, *_: (doc, pair, 0, 0),
            ),
            lanes_of(grads),
        ],
        [
            out_whole((docs, rows, width), BF16),
            out_whole((kept, docs, size + 8, width), F32),
            out_whole((blocks - kept, docs, size + 8, width), BF16),
            out_whole((kept, docs, size + 8, width), F32),
            out_whole((blocks - kept, docs, size + 8, width), BF16),
        ],
        [pltpu.VMEM((PAIRS, 2, count + 8, LANES), F32)],
    )


def feed_body(
    place, summed, cotangent, we, be, wr, br, ng, ns, fg, fs, wpo,
    outputs_far, normed_low, hidden, grad_branch, grad_pre, grad_summed_far, grad_second,
    grad_mix_far, vec, vec_wide,
    normed, slope, work, unit, outputs, grad_mix, sems,
):
    docs, rows = cotangent.shape[0], cotangent.shape[1]
    width = summed.shape[2]
    wide = we.shape[1]
    steps = rows // ROWS
    blocks = [
        (doc, step * ROWS, doc * rows + step * ROWS)
        for doc in range(docs)
        for step in range(steps)
    ]
    leaving = []

    def leave(source, target, doc, start, row):
        copy = pltpu.make_async_copy(
            source.at[pl.ds(row, ROWS)],
            target.at[doc, pl.ds(start, ROWS)],
            sems.at[len(leaving)],
        )
        copy.start()
        leaving.append(copy)


    def normal(value):
        centred = value - jnp.mean(value, axis=-1, keepdims=True)
        scale = lax.rsqrt(jnp.mean(centred * centred, axis=-1, keepdims=True) + EPSILON)
        return centred * scale, scale

    scales = []
    for doc, start, row in blocks:
        norm, scale = normal(summed[doc, start : start + ROWS])
        scales.append(scale)
        unit[row : row + ROWS] = norm
        full = norm * ng[...] + ns[...]
        normed[row : row + ROWS] = full
        normed_low[row : row + ROWS] = full.astype(BF16)

    def expand(index):
        part = slice(index * CHUNK, (index + 1) * CHUNK)
        pre = nn(normed_low[...], we[:, part]) + be[:, part]
        cdf = 0.5 * (1.0 + lax.erf(pre * math.sqrt(0.5)))
        hidden[:, part] = (pre * cdf).astype(BF16)
        slope[:, part] = cdf + pre * (jnp.exp(pre * pre * -0.5) * (1.0 / math.sqrt(2.0 * math.pi)))
    for index in range(wide // CHUNK):
        expand(index)

    for start in range(0, width, CHUNK):
        part = slice(start, start + CHUNK)
        work[:, part] = normed[:, part] + (nn(hidden[...], wr[:, part]) + br[:, part])

    sums = [jnp.zeros((1, width), F32) for _ in range(6)]
    for doc, start, row in blocks:
        norm, scale = normal(work[row : row + ROWS])
        spot = place[0] + start + positions((ROWS, 1), 0)
        valid = (spot < place[1 + doc]).astype(F32)
        outputs[row : row + ROWS] = (valid * (norm * fg[...] + fs[...])).astype(BF16)
        leave(outputs, outputs_far, doc, start, row)
        error = valid * cotangent[doc, start : start + ROWS].astype(F32)
        sums[0] += column_sum(error * norm)
        sums[1] += column_sum(error)
        scaled = error * fg[...]
        rest = (
            scaled
            - jnp.mean(scaled, axis=-1, keepdims=True)
            - norm * jnp.mean(scaled * norm, axis=-1, keepdims=True)
        ) * scale
        work[row : row + ROWS] = rest
        low = rest.astype(BF16)
        grad_branch[row : row + ROWS] = low
        sums[2] += column_sum(low)

    def reduce(index):
        part = slice(index * CHUNK, (index + 1) * CHUNK)
        low = (nt(grad_branch[...], wr[part, :]) * slope[:, part]).astype(BF16)
        grad_pre[:, part] = low
        vec_wide[:, part] = column_sum(low)

    for index in range(wide // CHUNK):
        reduce(index)

    for start in range(0, width, CHUNK):
        part = slice(start, start + CHUNK)
        work[:, part] += nt(grad_pre[...], we[part, :])

    for (doc, start, row), scale in zip(blocks, scales):
        error = work[row : row + ROWS]
        norm = unit[row : row + ROWS]
        sums[3] += column_sum(error * norm)
        sums[4] += column_sum(error)
        scaled = error * ng[...]
        grad = (
            scaled
            - jnp.mean(scaled, axis=-1, keepdims=True)
            - norm * jnp.mean(scaled * norm, axis=-1, keepdims=True)
        ) * scale
        unit[row : row + ROWS] = grad
        leave(unit, grad_summed_far, doc, start, row)
        low = grad.astype(BF16)
        grad_second[row : row + ROWS] = low
        sums[5] += column_sum(low)
        grad_mix[row : row + ROWS] = nt(low, wpo[...]).astype(BF16)
        leave(grad_mix, grad_mix_far, doc, start, row)
    for index, value in enumerate(sums):
        vec[index : index + 1] = value
    vec[6:8] = jnp.zeros((2, width), F32)
    for copy in leaving:
        copy.wait()


def feed(place, summed, cotangent, we, be, wr, br, ng, ns, fg, fs, wpo):
    docs, rows, width = summed.shape
    wide = we.shape[1]
    tokens = docs * rows
    return call(
        feed_body,
        (1,),
        (place,),
        [whole(a) for a in (summed, cotangent, we, be, wr, br, ng, ns, fg, fs, wpo)],
        [
            out_raw((docs, rows, width), BF16),
            out_whole((tokens, width), BF16),
            out_whole((tokens, wide), BF16),
            out_whole((tokens, width), BF16),
            out_whole((tokens, wide), BF16),
            out_raw((docs, rows, width), F32),
            out_whole((tokens, width), BF16),
            out_raw((docs, rows, width), BF16),
            out_whole((8, width), F32),
            out_whole((1, wide), F32),
        ],
        [
            pltpu.VMEM((tokens, width), F32),
            pltpu.VMEM((tokens, wide), F32),
            pltpu.VMEM((tokens, width), F32),
            pltpu.VMEM((tokens, width), F32),
            pltpu.VMEM((tokens, width), BF16),
            pltpu.VMEM((tokens, width), BF16),
            pltpu.SemaphoreType.DMA((3 * tokens // ROWS,)),
        ],
        spare=12,
    )


def key_value_body(place, *refs, docs):
    gk_kept, gk_came, gv_kept, gv_came, kx, vx, ck, cv = refs[:8]
    own, from_left, from_right, dq = refs[8:12]
    gk, gv, vec, rows_in, pooled, total = refs[12:]
    offset = place[0]
    rows, width = gk.shape[0] // docs, gk.shape[1]
    count = rows // STRIDE
    vec[...] = jnp.zeros_like(vec)
    for doc in range(docs):
        length = place[1 + doc]
        spot = offset - HALF + positions((rows + WIN, 1), 0)
        valid = (spot >= 0) & (spot < length)
        first = doc * rows
        for which, (kept, came, ext, taps, out, row) in enumerate(
            (
                (gk_kept, gk_came, kx, ck, gk, 0),
                (gv_kept, gv_came, vx, cv, gv, KER),
            )
        ):
            pooled[...] = kept[doc].astype(F32) + came[doc].astype(F32)
            masked = jnp.where(valid, ext[doc].astype(F32), 0.0)
            for group in range(width // LANES):
                lanes = slice(group * LANES, (group + 1) * LANES)
                grown = pooled[:count, lanes]
                shifted = pooled[1 : count + 1, lanes]
                rows_in[group] = masked[:, lanes]
                for tap in range(KER):
                    start = HALF - KER // 2 + tap
                    read = rows_in[group, pl.ds(start, count, stride=STRIDE), :]
                    vec[row + tap : row + tap + 1, lanes] += column_sum(grown * read)
                if which == 1:
                    vec[2 * KER : 2 * KER + 1, lanes] += column_sum(grown)
                total[group] = own[doc, which, :, lanes]
                total[group, :HALF] += from_left[doc, which, :, lanes].astype(F32)
                total[group, rows - HALF :] += from_right[doc, which, :, lanes].astype(F32)
                for phase, terms in enumerate(
                    (
                        ((2, grown),),
                        ((3, grown),),
                        ((4, grown), (0, shifted)),
                        ((1, shifted),),
                    )
                ):
                    part = pl.ds(phase, count, stride=STRIDE)
                    added = None
                    for tap, values in terms:
                        term = values * taps[tap : tap + 1, lanes]
                        added = term if added is None else added + term
                    inside = offset + phase + STRIDE * positions((count, 1), 0) < length
                    total[group, part, :] = total[group, part, :] + jnp.where(inside, added, 0.0)
                out[first : first + rows, lanes] = total[group].astype(BF16)
        vec[11:12] += column_sum(dq[doc])
    vec[12:13] += column_sum(gv[...])


def key_value_gradients(place, pooled_grads, kx, vx, ck, cv, own, left, right, dq):
    docs, rows, width = dq.shape
    return call(
        functools.partial(key_value_body, docs=docs),
        (1,),
        (place,),
        [
            whole(a)
            for a in (*pooled_grads, kx, vx, ck, cv, own, left, right, dq)
        ],
        [out_whole((docs * rows, width), BF16)] * 2 + [out_whole((16, width), F32)],
        [
            pltpu.VMEM((width // LANES, rows + WIN, LANES), F32),
            pltpu.VMEM((rows // STRIDE + 8, width), F32),
            pltpu.VMEM((width // LANES, rows, LANES), F32),
        ],
    )


def input_body(place, dq, gk, gv, gmid, wq, wk, wv, dx):
    total = nt(dq[...], wq[...]) + nt(gk[...], wk[...]) + nt(gv[...], wv[...])
    dx[...] = (gmid[...] + total.reshape(gmid.shape)).astype(BF16)


def input_gradient(place, dq, gk, gv, gmid, wq, wk, wv):
    docs, rows, width = gmid.shape
    (dx,) = call(
        input_body,
        (1,),
        (place,),
        [whole(a) for a in (dq, gk, gv, gmid, wq, wk, wv)],
        [out_whole((docs, rows, width), BF16)],
    )
    return dx


def scatter_body(bits, *refs, kinds, order, vectors, quartered):
    count = len(kinds)
    operands = [refs[2 * index : 2 * index + 2] for index in range(count)]
    extra = refs[2 * count : 2 * count + vectors]
    rest = refs[2 * count + vectors :]
    if quartered:
        results, (ordered, rounded, *small) = (rest[0], rest[0]), rest[1:]
    else:
        results, (ordered, rounded, *small) = rest[:2], rest[2:]
    core = bits[0]
    sides = 2 if ("batch", 1) in order else 1
    owners = 8

    def start_of(which, size):
        if quartered:
            return which * size
        return pl.multiple_of((which ^ core) * size, LANES)

    def place_tile(which, side, owner, target, size, value):
        index = []
        for at, (axis, bit) in enumerate(order):
            if axis == "batch":
                index += [side, which] if quartered else [side ^ bits[1 + at]]
            else:
                index.append(((owner >> bit) & 1) ^ bits[1 + at])
        results[which][(*index, slice(target, target + size), slice(None))] = value

    base = 0
    for (left, right), kind in zip(operands, kinds):
        tall = left.shape[1]
        turned = left[...].T
        if kind == "wide":
            half = right.shape[1] // 2
            size = tall // owners // sides
            for which in range(2):
                start = start_of(which, half)
                for part in range(half // 768):
                    rounded[...] = nn(turned, right[:, pl.ds(start + part * 768, 768)]).astype(BF16)
                    for column in range(2):
                        target = base + (2 * part + column) * size
                        for owner in range(owners):
                            for side in range(sides):
                                row = (owner * sides + side) * size
                                value = rounded[row : row + size, column * 384 : column * 384 + 384]
                                place_tile(which, side, owner, target, size, value)
            base += half // 384 * size
        elif kind == "tall":
            ordered[...] = turned
            size = tall // 2 // sides
            for part in range(right.shape[1] // 768):
                product = nn(ordered[...], right[:, part * 768 : part * 768 + 768])
                rounded[...] = product.astype(BF16)
                for column in range(2):
                    owner = 2 * part + column
                    for side in range(sides):
                        for which in range(2):
                            row = start_of(which, 384) + side * size
                            value = rounded[pl.ds(row, size), column * 384 : column * 384 + 384]
                            place_tile(which, side, owner, base, size, value)
            base += size
        else:
            size = tall // owners // sides
            if quartered:
                columns = right[...]
            else:
                columns = jnp.concatenate(
                    [right[:, pl.ds(start_of(which, 384), 384)] for which in range(2)], axis=1
                )
            rounded[...] = nn(turned, columns).astype(BF16)
            for which in range(2):
                for owner in range(owners):
                    for side in range(sides):
                        row = (owner * sides + side) * size
                        value = rounded[row : row + size, which * 384 : which * 384 + 384]
                        place_tile(which, side, owner, base, size, value)
            base += size
    if vectors:
        (block,) = small
        vec_feed, vec_first, vec_input, vec_wide = extra
        for owner in range(owners):
            lanes = slice(owner * 96, owner * 96 + 96)
            block[0, owner] = jnp.zeros(block.shape[2:], F32)
            block[1, owner] = jnp.zeros(block.shape[2:], F32)
            block[0, owner, 0:8, 0:96] = vec_feed[:, lanes]
            block[0, owner, 0:8, LANES : LANES + 96] = vec_first[:, lanes]
            block[1, owner, 0:16, 0:96] = vec_input[:, lanes]
            for part in range(4):
                at = owner * 384 + part * 96
                block[0, owner, 8 + part : 9 + part, 0:96] = vec_wide[:, at : at + 96]
        for owner in range(owners):
            for which in range(2):
                place_tile(which, 0, owner, base, 16, block[which ^ core, owner].astype(BF16))


def scatter_products(bits, order, items, extra=(), quartered=False):
    sides = 2 if ("batch", 1) in order else 1
    rows = 0
    for kind, left, right in items:
        if kind == "wide":
            rows += right.shape[1] // 768 * (left.shape[1] // 8 // sides)
        elif kind == "tall":
            rows += 384 // sides
        else:
            rows += 96 // sides
    rows += 16 if extra else 0
    shape = (2,) * (len(order) + quartered) + (rows, 384)
    operands = [array for _, left, right in items for array in (left, right)]
    return call(
        functools.partial(
            scatter_body,
            kinds=tuple(kind for kind, _, _ in items),
            order=tuple(order),
            vectors=len(extra),
            quartered=quartered,
        ),
        (1,),
        (bits,),
        [whole(a) for a in (*operands, *extra)],
        [out_whole(shape, BF16)] * (1 if quartered else 2),
        [pltpu.VMEM((768, operands[0].shape[0]), BF16), pltpu.VMEM((768, 768), BF16)]
        + ([pltpu.VMEM((2, 8, 16, 384), F32)] if extra else []),
    )


def quarter_products_body(bits, *refs, kinds, levels):
    count = len(kinds)
    operands = [refs[2 * index : 2 * index + 2] for index in range(count)]
    out, turned, by_owner, by_half, sems = refs[2 * count :]
    sides, cores, owners = 2, 2, 1 << levels
    pending = {}
    turns = {}

    def digits(owner):
        return tuple(((owner >> level) & 1) ^ bits[level] for level in range(levels))

    def next_slot(buffer):
        slot = turns.get(buffer, 0) % 2
        turns[buffer] = turns.get(buffer, 0) + 1
        for copy in pending.pop((buffer, slot), []):
            copy.wait()
        return slot

    def leave(buffer, slot, source, target):
        copies = pending.setdefault((buffer, slot), [])
        copy = pltpu.make_async_copy(source, target, sems.at[buffer, slot, len(copies)])
        copy.start()
        copies.append(copy)

    def spread_rows(value):
        slot = next_slot(0)
        size = 768 // owners // sides
        for owner in range(owners):
            for side in range(sides):
                row = (owner * sides + side) * size
                for column in range(2):
                    part = value[row : row + size, column * 384 : column * 384 + 384]
                    by_owner[(slot, column, side, *digits(owner))] = part
        return slot

    def leave_rows(slot, column, which, base):
        middle = (slice(None),) * levels
        leave(0, slot, by_owner.at[slot, column], out.at[(slice(None), which, *middle, pl.ds(base, 48))])

    base = 0
    for (left, right), kind in zip(operands, kinds):
        turned[...] = left[...].T
        if kind == "wide":
            for which in range(cores):
                for part in range(2):
                    start = which * 1536 + part * 768
                    value = nn(turned[...], right[:, start : start + 768]).astype(BF16)
                    slot = spread_rows(value)
                    for column in range(2):
                        leave_rows(slot, column, which, base + (2 * part + column) * 48)
            base += 192
        elif kind == "tall":
            for part in range(4):
                value = nn(turned[...], right[:, part * 768 : part * 768 + 768]).astype(BF16)
                slot = next_slot(1)
                for which in range(cores):
                    for side in range(sides):
                        row = (which * sides + side) * 192
                        for column in range(2):
                            part_value = value[row : row + 192, column * 384 : column * 384 + 384]
                            by_half[slot, column, side, which] = part_value
                for column in range(2):
                    owner = digits(2 * part + column)
                    target = out.at[(slice(None), slice(None), *owner, pl.ds(base, 192))]
                    leave(1, slot, by_half.at[slot, column], target)
            base += 192
        else:
            slot = spread_rows(nn(turned[...], right[...]).astype(BF16))
            for which in range(cores):
                leave_rows(slot, which, which, base)
            base += 48
    for copies in pending.values():
        for copy in copies:
            copy.wait()


def quarter_products(bits, items, levels):
    rows = sum(48 if kind == "square" else 192 for kind, _, _ in items)
    operands = [array for _, left, right in items for array in (left, right)]
    (out,) = call(
        functools.partial(
            quarter_products_body, kinds=tuple(kind for kind, _, _ in items), levels=levels
        ),
        (1,),
        (bits,),
        [whole(a) for a in operands],
        [out_raw((2, 2) + (2,) * levels + (rows, 384), BF16)],
        [
            pltpu.VMEM((768, operands[0].shape[0]), BF16),
            pltpu.VMEM((2, 2, 2) + (2,) * levels + (48, 384), BF16),
            pltpu.VMEM((2, 2, 2, 2, 192, 384), BF16),
            pltpu.SemaphoreType.DMA((2, 2, 2)),
        ],
    )
    return out


def order_quarters(spots, low, other, across, quarters):
    odd, upper = spots[0], spots[1]
    quarters[odd, upper] = low[...]
    quarters[odd, 1 - upper] = other[...]
    quarters[1 - odd, upper] = across[0]
    quarters[1 - odd, 1 - upper] = across[1]


def join_square(quarters, start, out):
    for core in range(2):
        for side in range(2):
            block = quarters[core, side, start : start + 48]
            out[side * 48 : side * 48 + 48, core * 384 : core * 384 + 384] = block.astype(F32)


def collect_feed_body(spots, low, other, across, expand, reduce, pooled_out, quarters, tall):
    order_quarters(spots, low, other, across, quarters)
    for core in range(2):
        for side in range(2):
            rows = slice(side * 48, side * 48 + 48)
            for part in range(4):
                column = core * 1536 + part * 384
                block = quarters[core, side, part * 48 : part * 48 + 48]
                expand[rows, column : column + 384] = block.astype(F32)
            at = core * 384 + side * 192
            tall[at : at + 192] = quarters[core, side, 192:384].astype(F32)
    reduce[...] = tall[...].T
    join_square(quarters, 384, pooled_out)


def collect_feed(spots, low, other, across):
    return call(
        collect_feed_body,
        (1,),
        (spots,),
        [whole(low), whole(other), whole(across)],
        [out_whole((96, 3072), F32), out_whole((384, 768), F32), out_whole((96, 768), F32)],
        [pltpu.VMEM((2, 2) + low.shape, BF16), pltpu.VMEM((768, 384), F32)],
    )


def collect_last_body(spots, low, other, across, *refs, cut):
    pq, lo, lq, lk, lv, vectors, quarters = refs
    order_quarters(spots, low, other, across, quarters)
    for index, out in enumerate((pq, lo, lq)):
        join_square(quarters, index * 48, out)
    for core in range(2):
        half = quarters[core, 0, cut:].astype(F32) + quarters[core, 1, cut:].astype(F32)
        lk[:, core * 384 : core * 384 + 384] = half[:96]
        lv[:, core * 384 : core * 384 + 384] = half[96:192]
        vectors[core] = half[192:208]


def collect_last(spots, low, other, across, cut):
    return call(
        functools.partial(collect_last_body, cut=cut),
        (1,),
        (spots,),
        [whole(low), whole(other), whole(across)],
        [out_whole((96, 768), F32)] * 5 + [out_whole((2, 16, 384), F32)],
        [pltpu.VMEM((2, 2) + low.shape, BF16)],
    )


def swap(value, axis, bit):
    count = lax.axis_size(axis)
    return lax.ppermute(value, axis, [(i, i ^ (1 << bit)) for i in range(count)])


def shift(value, axis, by):
    count = lax.axis_size(axis)
    pairs = [(i, i + by) for i in range(count) if 0 <= i + by < count]
    return lax.ppermute(value, axis, pairs)


def fold(kept, came):
    low = (kept[1].astype(F32) + came[1].astype(F32)).astype(BF16)
    return low, kept[0].astype(F32) + came[0].astype(F32)


def total_of(terms, *index):
    total = None
    for term in terms:
        value = term[index].astype(F32)
        total = value if total is None else total + value
    return total


def advance(terms, hop):
    came = swap(total_of(terms, 1).astype(BF16), *hop)
    return [term[0] for term in terms], came


def cut(quarters, start, size):
    return quarters[:, :, start : start + size]


def device_step(
    inputs, lengths, cotangent,
    local_query, local_query_bias, local_key, local_value, local_value_bias,
    local_output, local_output_bias, pooled_query, pooled_query_bias,
    pooled_output, pooled_output_bias, conv_key, conv_value, conv_value_bias,
    norm_gain, norm_shift, expand_weight, expand_bias, reduce_weight, reduce_bias,
    final_gain, final_shift,
):
    docs, rows, width = inputs.shape
    devices = lax.axis_size("seq")
    me = lax.axis_index("seq")
    mine = lax.axis_index("batch")
    levels = devices.bit_length() - 1
    size = rows // STRIDE
    flat = docs * rows
    offset = me * rows
    reach = -(-REACH // size)
    gathered = devices <= 2 * reach
    fast = devices == 8 and width == 768 and lax.axis_size("batch") == 4
    base = jnp.where(gathered, 0, offset // STRIDE - reach * size)
    place = jnp.concatenate([offset[None], lengths, base[None]]).astype(jnp.int32)

    def line(vector):
        return vector[None]

    def tokens(array):
        return array.reshape(flat, array.shape[-1])

    taps_key, taps_value = conv_key.T, conv_value.T

    left = shift(inputs[:, rows - HALF :], "seq", 1)
    right = shift(inputs[:, :HALF], "seq", -1)
    q, k_own, v_own, key_near, value_near = project(
        place, inputs, local_query, line(local_query_bias), local_key, local_value,
        line(local_value_bias),
    )
    left, right, k_own = sync(left, right, k_own)
    kx, vx, pooled = pool(
        place, left, right, k_own, v_own, key_near, value_near, line(local_value_bias),
        taps_key, taps_value, line(conv_value_bias),
    )
    own = [pooled[which][None] for which in range(2)]

    mixes, probs_one = [], []

    def local_step(doc, token):
        mix, probs = local_forward(token, q, kx, vx, doc)
        mixes.append(mix)
        probs_one.append(probs)
        return mix

    if gathered:
        orders = ([2, 1, 0], [0, 2, 1]) if levels == 3 else (list(range(levels)),) * 2
        have = own
        pieces = [[own[0]], [own[1]]]
        relative = [[0], [0]]
        token = place
        for stage in range(levels):
            came = [swap(have[which], "seq", orders[which][stage]) for which in range(2)]
            if stage == 0:
                came[0], came[1], token = sync(came[0], came[1], token)
            if 0 < stage <= docs:
                done = local_step(stage - 1, token)
            if stage == levels - 1:
                while len(mixes) < docs:
                    local_step(len(mixes), token)
                mix_one, middle, middle_low, q2 = middle_forward(
                    token, inputs, local_output, line(local_output_bias), pooled_query,
                    line(pooled_query_bias), mixes,
                )
                came[0], came[1], q2, token = sync(came[0], came[1], q2, token)
            elif stage > 0:
                came[0], came[1], mixes[stage - 1], token = sync(
                    came[0], came[1], done, token
                )
            for which in range(2):
                pieces[which].append(came[which])
                relative[which] += [r ^ (1 << orders[which][stage]) for r in relative[which]]
                if stage < levels - 1:
                    have[which] = jnp.concatenate([have[which], came[which]])
        slots = jnp.stack([me ^ jnp.array(r, jnp.int32) for r in relative])
    else:
        pieces = [
            [own[which]]
            + [
                shift(own[which], "seq", sign * distance)
                for distance in range(1, reach + 1)
                for sign in (1, -1)
            ]
            for which in range(2)
        ]
        spots = [reach] + [
            reach - sign * distance for distance in range(1, reach + 1) for sign in (1, -1)
        ]
        slots = jnp.array([spots, spots], jnp.int32)
        token = place
        for doc in range(docs):
            local_step(doc, token)
        mix_one, middle, middle_low, q2 = middle_forward(
            token, inputs, local_output, line(local_output_bias), pooled_query,
            line(pooled_query_bias), mixes,
        )

    keys, values, probs_two, mix_two, summed, expand_near, reduce_near = pooled_forward(
        token, slots, pieces[0], pieces[1], q2, middle, pooled_output, line(pooled_output_bias),
        expand_weight, reduce_weight,
    )
    (
        outputs, normed_low, hidden, grad_branch, grad_pre, grad_summed, grad_second, grad_mix_two,
        vec_feed, vec_wide,
    ) = feed(
        token, summed, cotangent, expand_near, line(expand_bias), reduce_near,
        line(reduce_bias), line(norm_gain), line(norm_shift), line(final_gain),
        line(final_shift), pooled_output,
    )

    order_first = [("batch", 1)] + [("seq", level) for level in range(levels)]
    order_last = order_first[1:]

    def bits_of(order):
        ids = [mine & 1] + [(mine if axis == "batch" else me) >> bit & 1 for axis, bit in order]
        return jnp.stack(ids).astype(jnp.int32)

    seq_bits = jnp.stack([me >> level & 1 for level in range(levels)]).astype(jnp.int32)

    def over_batch(blocks):
        part = blocks.shape[2:]
        flat_blocks = blocks.reshape(-1, blocks.shape[-1])
        mine_part = lax.psum_scatter(flat_blocks, "batch", scatter_dimension=0, tiled=True)
        return mine_part.reshape(part)

    if fast:
        feed_blocks = quarter_products(
            seq_bits,
            [
                ("wide", normed_low, grad_pre),
                ("tall", grad_branch, hidden),
                ("square", tokens(mix_two), grad_second),
            ],
            levels,
        )
        feed_blocks, grad_mix_two, token = sync(feed_blocks, grad_mix_two, token)
        feed_part = over_batch(feed_blocks)

    blocks = devices if gathered else 2 * reach + 1
    if gathered:
        back = ([0, 1, 2], [1, 2, 0]) if levels == 3 else (list(range(levels)),) * 2
        places = []
        for which in range(2):
            spots = []
            for block in range(devices):
                relative = 0
                for at, bit in enumerate(back[which]):
                    relative |= (block >> (levels - 1 - at) & 1) << bit
                spots.append(relative)
            places.append(me ^ jnp.array(spots, jnp.int32))
        places = jnp.stack(places)
        half_blocks = devices // 2
    else:
        middle_first = [reach] + [spot for spot in range(blocks) if spot != reach]
        places = jnp.array([middle_first, middle_first], jnp.int32)
        half_blocks = 1
    grad_q2, dk_kept, dk_sent, dv_kept, dv_sent = pooled_backward(
        places, token, q2, keys, values, probs_two, grad_mix_two, size, half_blocks
    )
    grad_middle, grad_first, grad_mix_one, vec_first = first_backward(
        token, grad_q2, grad_summed, pooled_query, local_output
    )
    back_parts = ()

    def back_step(doc, token):
        return local_backward(
            token, q, kx, vx, grad_mix_one, probs_one[doc], doc, back_parts
        )

    if gathered:
        kept = [part.reshape((2,) * (levels - 1) + part.shape[1:]) for part in (dk_kept, dv_kept)]
        sent = [part.reshape((2,) * (levels - 1) + part.shape[1:]) for part in (dk_sent, dv_sent)]
        for stage in range(levels):
            came = [swap(sent[which], "seq", back[which][stage]) for which in range(2)]
            if stage < docs:
                back_parts = list(back_step(stage, token))
            if stage == docs - 1:
                from_left = shift(back_parts[3], "seq", 1)
                from_right = shift(back_parts[2], "seq", -1)
            if fast and stage == 0:
                came[0], came[1], back_parts[0], token = sync(
                    came[0], came[1], back_parts[0], token
                )
            if fast and stage == 1:
                came[0], came[1], from_left, from_right, token = sync(
                    came[0], came[1], from_left, from_right, token
                )
            if fast and stage == 2:
                middle_kept, middle_sent = scatter_products(
                    bits_of(order_first) + 0 * token[0],
                    order_first,
                    [
                        ("square", tokens(middle_low), tokens(grad_q2)),
                        ("square", tokens(mix_one), grad_first),
                        ("square", tokens(inputs), tokens(back_parts[0])),
                    ],
                )
                came[0], came[1], middle_sent, token = sync(
                    came[0], came[1], middle_sent, token
                )
            if stage < levels - 1:
                for which in range(2):
                    sent[which], kept[which] = fold(kept[which], came[which])
        pooled_grads = [kept[0], came[0], kept[1], came[1]]
    else:
        pooled_grads = []
        for kept, sent in ((dk_kept, dk_sent), (dv_kept, dv_sent)):
            total = kept[0]
            for distance in range(1, reach + 1):
                total = total + shift(sent[reach - distance], "seq", -distance).astype(F32)
                total = total + shift(sent[reach + distance - 1], "seq", distance).astype(F32)
            after = shift(total[:, :1].astype(BF16), "seq", -1).astype(F32)
            total = jnp.concatenate([total[:, :size], jnp.tile(after, (1, 8, 1))], axis=1)
            pooled_grads += [total, jnp.zeros_like(total)]
        for doc in range(docs):
            back_parts = back_step(doc, token)
        from_left = shift(back_parts[3], "seq", 1)
        from_right = shift(back_parts[2], "seq", -1)
    dq, own_grads = back_parts[:2]
    if fast:
        middle_came = swap(middle_sent, "batch", 0)
    grad_k, grad_v, vec_input = key_value_gradients(
        token, pooled_grads, kx, vx, taps_key, taps_value,
        own_grads, from_left, from_right, dq,
    )
    if fast:
        last_kept, last_sent = scatter_products(
            bits_of(order_last),
            order_last,
            [("square", tokens(inputs), grad_k), ("square", tokens(inputs), grad_v)],
            (vec_feed, vec_first, vec_input, vec_wide),
        )
        last_sent, middle_came, token = sync(last_sent, middle_came, token)
        last_came = swap(last_sent, "batch", 0)
        middle_terms, middle_came = advance([middle_kept, middle_came], ("batch", 1))
    input_grad = input_gradient(
        token, tokens(dq), grad_k, grad_v, grad_middle, local_query, local_key, local_value
    )

    if fast:
        cut_feed = feed_part.shape[-2] // 2
        one = [feed_part[..., :cut_feed, :]]
        two = [feed_part[..., cut_feed:, :]]

        def advance_second(terms, hop):
            came = swap(total_of(terms, slice(None), 1).astype(BF16), *hop)
            return [term[:, 0] for term in terms], came

        one, one_came = advance(one, ("seq", 0))
        two, two_came = advance_second(two, ("seq", 1))
        input_grad, last_came, middle_came, one_came, two_came = sync(
            input_grad, last_came, middle_came, one_came, two_came
        )
        last_terms, last_came = advance([last_kept, last_came], ("seq", 0))
        middle_terms, middle_came = advance_second(middle_terms + [middle_came], ("seq", 1))
        one, one_came = advance(one + [one_came], ("seq", 1))
        two, two_came = advance(two + [two_came], ("seq", 0))
        last_came, middle_came, one_came, two_came = sync(
            last_came, middle_came, one_came, two_came
        )

        last_terms, last_came = advance(last_terms + [last_came], ("seq", 1))
        one, two = one + [one_came], two + [two_came]
        feed_came = swap(
            jnp.concatenate([total_of(one, 1), total_of(two, 1)]).astype(BF16), "seq", 2
        )
        middle_terms, middle_came = advance(middle_terms + [middle_came], ("seq", 0))
        last_came, middle_came, feed_came = sync(last_came, middle_came, feed_came)

        last_terms, last_came = advance(last_terms + [last_came], ("seq", 2))
        middle_terms, middle_came = advance(middle_terms + [middle_came], ("seq", 2))
        feed_low = (
            jnp.concatenate([total_of(one, 0), total_of(two, 0)]) + feed_came.astype(F32)
        ).astype(BF16)
        feed_other = swap(feed_low, "batch", 1)
        last_came, middle_came, feed_other = sync(last_came, middle_came, feed_other)
        cut_at = middle_came.shape[0]
        low = jnp.concatenate(
            [
                total_of(middle_terms + [middle_came], Ellipsis),
                total_of(last_terms + [last_came], Ellipsis),
            ]
        ).astype(BF16)
        other = swap(low, "batch", 1)
        feed_across = swap(jnp.stack([feed_low, feed_other]), "batch", 0)
        low, other, feed_across = sync(low, other, feed_across)
        across = swap(jnp.stack([low, other]), "batch", 0)
        spots = jnp.stack([mine & 1, mine >> 1]).astype(jnp.int32)
        grad_expand, grad_reduce, grad_po = collect_feed(spots, feed_low, feed_other, feed_across)
        grad_pq, grad_lo, grad_lq, grad_lk, grad_lv, lines = collect_last(
            spots, low, other, across, cut_at
        )
        vec_low, vec_high = lines[0, :, :96], lines[1, :, :96]
        (fg, fs, rb, ng, ns, pob) = [vec_low[index] for index in range(6)]
        pqb, lob = lines[0, 0, LANES : LANES + 96], lines[0, 1, LANES : LANES + 96]
        grad_eb = vec_low[8:12].reshape(-1)
    else:

        def plain(left_array, right_array):
            product = tn(left_array, right_array)
            part = lax.psum_scatter(product, "seq", scatter_dimension=0, tiled=True)
            return lax.psum(part.astype(BF16), "batch").astype(F32)

        grad_expand = plain(normed_low, grad_pre)
        grad_reduce = plain(hidden, grad_branch)
        grad_po = plain(tokens(mix_two), grad_second)
        grad_pq = plain(tokens(middle_low), tokens(grad_q2))
        grad_lo = plain(tokens(mix_one), grad_first)
        grad_lq = plain(tokens(inputs), tokens(dq))
        grad_lk = plain(tokens(inputs), grad_k)
        grad_lv = plain(tokens(inputs), grad_v)
        vectors = jnp.concatenate(
            [vec_feed, vec_first, vec_input, vec_wide.reshape(-1, width)], axis=0
        )
        vectors = lax.psum(vectors, ("seq", "batch"))
        share = width // devices
        part = lax.dynamic_slice_in_dim(vectors, me * share, share, axis=1)
        wide = vectors[32:].reshape(-1)
        wide_share = wide.shape[0] // devices
        grad_eb = lax.dynamic_slice_in_dim(wide, me * wide_share, wide_share, axis=0)
        (fg, fs, rb, ng, ns, pob) = [part[index] for index in range(6)]
        pqb, lob = part[8], part[9]
        vec_high = part[16:32]
    grad_ck = vec_high[:KER].T
    grad_cv = vec_high[KER : 2 * KER].T
    cvb, lqb, lvb = vec_high[10], vec_high[11], vec_high[12]
    return (
        outputs, input_grad,
        grad_lq, lqb, grad_lk, grad_lv, lvb, grad_lo, lob, grad_pq, pqb, grad_po, pob,
        grad_ck, grad_cv, cvb, ng, ns, grad_expand, grad_eb, grad_reduce, rb, fg, fs,
    )


def solution(mesh):
    vector = P("seq")
    matrix = P("seq", None)
    return jax.shard_map(
        device_step,
        mesh=mesh,
        in_specs=(P("batch", "seq", None), P("batch"), P("batch", "seq", None)) + (P(),) * 22,
        out_specs=(
            P("batch", "seq", None), P("batch", "seq", None),
            matrix, vector, matrix, matrix, vector, matrix, vector, matrix, vector, matrix, vector,
            matrix, matrix, vector, vector, vector, matrix, vector, matrix, vector, vector, vector,
        ),
        check_vma=False,
    )
```

profile of v0, /device:TPU:1, one launch (start us, length us, event | category | flops | bytes accessed | tf_op | source)
XLA Modules:
  0.0 329.2 jit_solution(7518262818730886136)
XLA Ops:
  8.3 4.0 %collective-permute-start = (bf16[2,64,768]{2,1,0:T(8,128)(2,1)S(1)}, bf16[2,64,768]{2,1,0:T(8,128)(2,1)S(1)}, u32[]{:S(2)}, u32[]{:S(2)}) collective-permute-start(bf16[2,64,768]{2,1,0:T(8,128)(2,1)S(1)} %get-tuple-element.275), channel_id=1, source_target_pairs={{0,4},{4,8},{8,12},{12,16},{16,20},{20,24},{24,28},{1,5},{5,9},{9,... | collective-permute-start | bytes 589832 | tf_op jit(solution)/shard_map/ppermute | solution.py:1093
  15.7 4.8 %shard_map.460 = (bf16[2,256,768]{2,1,0:T(8,128)(2,1)S(1)}, bf16[2,256,768]{2,1,0:T(8,128)(2,1)S(1)}, bf16[2,256,768]{2,1,0:T(8,128)(2,1)S(1)}, bf16[768,768]{1,0:T(8,128)(2,1)S(1)}, bf16[768,768]{1,0:T(8,128)(2,1)S(1)}) custom-call(s32[4]{0:T(128)S(1)} %pad_add_fusion.1.place.token, bf16[2,256,768]{2,1,0:T(8,128)(2,1)} %x.1, bf16[768,768]{1,0:T(8,128)(2,1)} %wq.1, ...), custom_call_target="tpu_custom_call" | custom-call | flops 1000 | bytes 1000 | tf_op jit(solution)/shard_map/pallas_call | solution.py:72
  22.6 4.7 %collective-permute-start.2 = (bf16[1,2,64,768]{3,2,1,0:T(8,128)(2,1)S(1)}, bf16[1,2,64,768]{3,2,1,0:T(8,128)(2,1)S(1)}, u32[]{:S(2)}, u32[]{:S(2)}) collective-permute-start(bf16[1,2,64,768]{3,2,1,0:T(8,128)(2,1)S(1)} %get-tuple-element.277.refs_0_), channel_id=1, source_target_pairs={{0,16},{4,20},{8,24},{12,28},{16,0},{20,4},{24,8},{28,12},{1,17},{... | collective-permute-start | bytes 589832 | tf_op jit(solution)/shard_map/ppermute | solution.py:1087
  27.3 8.9 %collective-permute-done.2.refs_1_ = bf16[1,2,64,768]{3,2,1,0:T(8,128)(2,1)S(1)} collective-permute-done((bf16[1,2,64,768]{3,2,1,0:T(8,128)(2,1)S(1)}, bf16[1,2,64,768]{3,2,1,0:T(8,128)(2,1)S(1)}, u32[]{:S(2)}, u32[]{:S(2)}) %collective-permute-start.2) | collective-permute-done | bytes 196640 | tf_op jit(solution)/shard_map/ppermute | solution.py:1087
  36.4 4.3 %collective-permute-start.4 = (bf16[2,2,64,768]{3,2,1,0:T(8,128)(2,1)S(1)}, bf16[2,2,64,768]{3,2,1,0:T(8,128)(2,1)S(1)}, u32[]{:S(2)}, u32[]{:S(2)}) collective-permute-start(bf16[2,2,64,768]{3,2,1,0:T(8,128)(2,1)S(1)} %pad_maximum_fusion.4), channel_id=1, source_target_pairs={{0,8},{4,12},{8,0},{12,4},{16,24},{20,28},{24,16},{28,20},{1,9},{5... | collective-permute-start | bytes 1179656 | tf_op jit(solution)/shard_map/ppermute | solution.py:1087
  40.7 4.8 %shard_map.462 = (bf16[256,768]{1,0:T(8,128)(2,1)S(1)}, f32[6,2,256,256]{3,2,1,0:T(8,128)S(1)}) custom-call(s32[4]{0:T(128)S(1)} %pad_add_fusion.1.place.token, bf16[2,256,768]{2,1,0:T(8,128)(2,1)S(1)} %get-tuple-element.152.q, bf16[2,384,768]{2,1,0:T(8,128)(2,1)S(1)} %get-tuple-element.153.kx.refs_4_, bf16[2,384,768]{2,1,0:T(8,128)(2,1)S(1)} %get-tuple-element.154.vx.refs_5_), custom_call_target="tpu_custom_call" | custom-call | flops 1000 | bytes 1000 | tf_op jit(solution)/shard_map/pallas_call | solution.py:72
  47.9 7.3 %collective-permute-done.5.refs_6_ = bf16[2,2,64,768]{3,2,1,0:T(8,128)(2,1)S(1)} collective-permute-done((bf16[2,2,64,768]{3,2,1,0:T(8,128)(2,1)S(1)}, bf16[2,2,64,768]{3,2,1,0:T(8,128)(2,1)S(1)}, u32[]{:S(2)}, u32[]{:S(2)}) %collective-permute-start.5) | collective-permute-done | bytes 393248 | tf_op jit(solution)/shard_map/ppermute | solution.py:1087
  61.5 4.8 %shard_map.463 = (bf16[256,768]{1,0:T(8,128)(2,1)S(1)}, f32[6,2,256,256]{3,2,1,0:T(8,128)S(1)}) custom-call(s32[4]{0:T(128)S(1)} %pad_add_fusion.1.place.token, bf16[2,256,768]{2,1,0:T(8,128)(2,1)S(1)} %copy-done.2, bf16[2,384,768]{2,1,0:T(8,128)(2,1)S(1)} %get-tuple-element.153.kx.refs_4_, bf16[2,384,768]{2,1,0:T(8,128)(2,1)S(1)} %get-tuple-element.154.vx.refs_5_), custom_call_target="tpu_custom_call" | custom-call | flops 1000 | bytes 1000 | tf_op jit(solution)/shard_map/pallas_call | solution.py:72
  74.4 24.3 %shard_map.465 = (bf16[2,512,768]{2,1,0:T(8,128)(2,1)}, bf16[2,512,768]{2,1,0:T(8,128)(2,1)}, f32[2,6,512,512]{3,2,1,0:T(8,128)}, bf16[2,256,768]{2,1,0:T(8,128)...) custom-call(s32[4]{0:T(128)S(1)} %pad_add_fusion.1.place.token, ...), custom_call_target="tpu_custom_call" | custom-call | flops 1000 | bytes 1000 | tf_op jit(solution)/shard_map/pallas_call | solution.py:72
  98.7 18.5 %shard_map.466 = (bf16[2,256,768]{2,1,0:T(8,128)(2,1)}, bf16[512,768]{1,0:T(8,128)(2,1)S(1)}, bf16[512,3072]{1,0:T(8,128)(2,1)S(1)}, bf16[512,768]{1,0:T(8,128)(...) custom-call(s32[4]{0:T(128)S(1)} %pad_add_fusion.1.place.token, ...), custom_call_target="tpu_custom_call" | custom-call | flops 1000 | bytes 1000 | tf_op jit(solution)/shard_map/pallas_call | solution.py:72
  117.3 10.5 %shard_map.467 = bf16[2,2,2,2,2,432,384]{6,5,4,3,2,1,0:T(8,128)(2,1)} custom-call(s32[3]{0:T(128)S(1)} %pad_add_fusion.3.bits, bf16[512,768]{1,0:T(8,128)(2,1)S(1)} %get-tuple-element.171.refs_0_, bf16[512,3072]{1,0:T(8,128)(2,1)S(1)} %get-tuple-element.172.refs_1_, bf16[512,768]{1,0:T(8,128)(2,1)S(1)} %get-tuple-element.173.refs_2_, ...), custom_call_target="tpu_custom_call" | custom-call | flops 1000 | bytes 1000 | tf_op jit(solution)/shard_map/pallas_call | solution.py:72
  128.5 14.4 %shard_map.468 = (bf16[2,256,768]{2,1,0:T(8,128)(2,1)S(1)}, f32[4,2,72,768]{3,2,1,0:T(8,128)S(1)}, bf16[4,2,72,768]{3,2,1,0:T(8,128)(2,1)S(1)}, f32[4,2,72,768]{3,2,1,0:T(8,128)S(1)}, bf16[4,2,72,768]{3,2,1,0:T(8,128)(2,1)S(1)}) custom-call(s32[2,8]{1,0:T(2,128)S(1)} %copy-done.73, s32[4]{0:T(128)S(1)} %pad_add_fusion.1.place.token, ...), custom_call_target="tpu_custom_call" | custom-call | flops 1000 | bytes 1000 | tf_op jit(solution)/shard_map/pallas_call | solution.py:72
  148.9 4.5 %shard_map.470 = (bf16[1,256,768]{2,1,0:T(8,128)(2,1)S(1)}, f32[1,2,256,768]{3,2,1,0:T(8,128)S(1)}, bf16[1,2,64,768]{3,2,1,0:T(8,128)(2,1)S(1)}, bf16[1,2,64,768]{3,2,1,0:T(8,128)(2,1)S(1)}) custom-call(s32[4]{0:T(128)S(1)} %pad_add_fusion.1.place.token, bf16[2,256,768]{2,1,0:T(8,128)(2,1)S(1)} %copy-done.3, ...), custom_call_target="tpu_custom_call" | custom-call | flops 1000 | bytes 1000 | tf_op jit(solution)/shard_map/pallas_call | solution.py:72
  153.4 7.3 %collective-permute-done.8 = bf16[2,2,2,72,768]{4,3,2,1,0:T(8,128)(2,1)S(1)} collective-permute-done((bf16[2,2,2,72,768]{4,3,2,1,0:T(8,128)(2,1)S(1)}, bf16[2,2,2,72,768]{4,3,2,1,0:T(8,128)(2,1)S(1)}, u32[]{:S(2)}, u32[]{:S(2)}) %collective-permute-start.8) | collective-permute-done | bytes 884768 | tf_op jit(solution)/shard_map/ppermute | solution.py:1087
  162.5 5.9 %collective-permute-start.11 = (bf16[2,2,72,768]{3,2,1,0:T(8,128)(2,1)S(1)}, bf16[2,2,72,768]{3,2,1,0:T(8,128)(2,1)S(1)}, u32[]{:S(2)}, u32[]{:S(2)}) collective-permute-start(bf16[2,2,72,768]{3,2,1,0:T(8,128)(2,1)S(1)} %get-tuple-element.267), channel_id=1, source_target_pairs={{0,16},{4,20},{8,24},{12,28},{16,0},{20,4},{24,8},{28,12},{1,17},{... | collective-permute-start | bytes 1327112 | tf_op jit(solution)/shard_map/ppermute | solution.py:1087
  170.3 4.6 %shard_map.471 = (bf16[2,256,768]{2,1,0:T(8,128)(2,1)S(1)}, f32[2,2,256,768]{3,2,1,0:T(8,128)S(1)}, bf16[2,2,64,768]{3,2,1,0:T(8,128)(2,1)S(1)}, bf16[2,2,64,768]{3,2,1,0:T(8,128)(2,1)S(1)}) custom-call(s32[4]{0:T(128)S(1)} %pad_add_fusion.1.place.token, bf16[2,256,768]{2,1,0:T(8,128)(2,1)S(1)} %copy-done.3, ...), custom_call_target="tpu_custom_call" | custom-call | flops 1000 | bytes 1000 | tf_op jit(solution)/shard_map/pallas_call | solution.py:72
  183.6 4.2 %collective-permute-done.13.refs_10_ = bf16[2,2,64,768]{3,2,1,0:T(8,128)(2,1)S(1)} collective-permute-done((bf16[2,2,64,768]{3,2,1,0:T(8,128)(2,1)S(1)}, bf16[2,2,64,768]{3,2,1,0:T(8,128)(2,1)S(1)}, u32[]{:S(2)}, u32[]{:S(2)}) %collective-permute-start.13) | collective-permute-done | bytes 393248 | tf_op jit(solution)/shard_map/ppermute | solution.py:1093
  189.6 10.4 %collective-permute-start.15 = (bf16[2,72,768]{2,1,0:T(8,128)(2,1)}, bf16[2,72,768]{2,1,0:T(8,128)(2,1)}, u32[]{:S(2)}, u32[]{:S(2)}) collective-permute-start(bf16[2,72,768]{2,1,0:T(8,128)(2,1)} %get-tuple-element.271), channel_id=1, source_target_pairs={{0,4},{4,0},{8,12},{12,8},{16,20},{20,16},{24,28},{28,24},{1,5},{5... | collective-permute-start | bytes 663560 | tf_op jit(solution)/shard_map/ppermute | solution.py:1087
  215.5 3.9 %shard_map.473 = (bf16[512,768]{1,0:T(8,128)(2,1)S(1)}, bf16[512,768]{1,0:T(8,128)(2,1)S(1)}, f32[16,768]{1,0:T(8,128)S(1)}) custom-call(s32[4]{0:T(128)S(1)} %pad_add_fusion.1.place.token, f32[2,72,768]{2,1,0:T(8,128)S(1)} %copy-done.35, bf16[2,72,768]{2,1,0:T(8,128)(2,1)} %collective-permute-done.14.refs_1_, f32[2,72,768]{2,1,0:T(8,128)S(1)} %copy-done.34, ...), custom_call_target="tpu_custom_call" | custom-call | flops 1000 | bytes 1000 | tf_op jit(solution)/shard_map/pallas_call | solution.py:72
  236.6 10.0 %collective-permute-done.18 = bf16[2,2,2,144,384]{4,3,2,1,0:T(8,128)(2,1)} collective-permute-done((bf16[2,2,2,144,384]{4,3,2,1,0:T(8,128)(2,1)}, bf16[2,2,2,144,384]{4,3,2,1,0:T(8,128)(2,1)}, u32[]{:S(2)}, u32[]{:S(2)}) %collective-permute-start.18) | collective-permute-done | bytes 884768 | tf_op jit(solution)/shard_map/ppermute | solution.py:1087
  252.6 14.8 %collective-permute-done.23 = bf16[2,216,384]{2,1,0:T(8,128)(2,1)S(1)} collective-permute-done((bf16[2,216,384]{2,1,0:T(8,128)(2,1)S(1)}, bf16[2,216,384]{2,1,0:T(8,128)(2,1)S(1)}, u32[]{:S(2)}, u32[]{:S(2)}) %collective-permute-start.23) | collective-permute-done | bytes 331808 | tf_op jit(solution)/shard_map/ppermute | solution.py:1087
  282.6 5.5 %collective-permute-done.27 = bf16[432,384]{1,0:T(8,128)(2,1)S(1)} collective-permute-done((bf16[432,384]{1,0:T(8,128)(2,1)S(1)}, bf16[432,384]{1,0:T(8,128)(2,1)S(1)}, u32[]{:S(2)}, u32[]{:S(2)}) %collective-permute-start.27) | collective-permute-done | bytes 331808 | tf_op jit(solution)/shard_map/ppermute | solution.py:1087
  293.7 9.9 %collective-permute-done.29 = bf16[144,384]{1,0:T(8,128)(2,1)S(1)} collective-permute-done((bf16[144,384]{1,0:T(8,128)(2,1)S(1)}, bf16[144,384]{1,0:T(8,128)(2,1)S(1)}, u32[]{:S(2)}, u32[]{:S(2)}) %collective-permute-start.29) | collective-permute-done | bytes 110624 | tf_op jit(solution)/shard_map/ppermute | solution.py:1087
  307.8 7.5 %collective-permute-done.31.other = bf16[352,384]{1,0:T(8,128)(2,1)S(1)} collective-permute-done((bf16[352,384]{1,0:T(8,128)(2,1)S(1)}, bf16[352,384]{1,0:T(8,128)(2,1)S(1)}, u32[]{:S(2)}, u32[]{:S(2)}) %collective-permute-start.31) | collective-permute-done | bytes 270368 | tf_op jit(solution)/shard_map/ppermute | solution.py:1087
  (293 shorter events, 114.3 us)
Async XLA Ops:
  7.2 219.2 %reduce-scatter.2.cloned.1.call-start = ((), (), s32[]{:S(2)}) async-start(), calls=%async_computation.1 | async-start | bytes 13271040 | tf_op jit(solution)/shard_map/reduce_scatter | solution.py:1246
  8.3 12.3 %collective-permute-start = (bf16[2,64,768]{2,1,0:T(8,128)(2,1)S(1)}, bf16[2,64,768]{2,1,0:T(8,128)(2,1)S(1)}, u32[]{:S(2)}, u32[]{:S(2)}) collective-permute-start(bf16[2,64,768]{2,1,0:T(8,128)(2,1)S(1)} %get-tuple-element.275), channel_id=1, source_target_pairs={{0,4},{4,8},{8,12},{12,16},{16,20},{20,24},{24,28},{1,5},{5,9},{9,... | collective-permute-start | bytes 589832 | tf_op jit(solution)/shard_map/ppermute | solution.py:1093
  22.6 13.6 %collective-permute-start.2 = (bf16[1,2,64,768]{3,2,1,0:T(8,128)(2,1)S(1)}, bf16[1,2,64,768]{3,2,1,0:T(8,128)(2,1)S(1)}, u32[]{:S(2)}, u32[]{:S(2)}) collective-permute-start(bf16[1,2,64,768]{3,2,1,0:T(8,128)(2,1)S(1)} %get-tuple-element.277.refs_0_), channel_id=1, source_target_pairs={{0,16},{4,20},{8,24},{12,28},{16,0},{20,4},{24,8},{28,12},{1,17},{... | collective-permute-start | bytes 589832 | tf_op jit(solution)/shard_map/ppermute | solution.py:1087
  36.3 18.9 %collective-permute-start.5 = (bf16[2,2,64,768]{3,2,1,0:T(8,128)(2,1)S(1)}, bf16[2,2,64,768]{3,2,1,0:T(8,128)(2,1)S(1)}, u32[]{:S(2)}, u32[]{:S(2)}) collective-permute-start(bf16[2,2,64,768]{3,2,1,0:T(8,128)(2,1)S(1)} %pad_maximum_fusion.5), channel_id=1, source_target_pairs={{0,16},{4,20},{8,24},{12,28},{16,0},{20,4},{24,8},{28,12},{1,17},{... | collective-permute-start | bytes 1179656 | tf_op jit(solution)/shard_map/ppermute | solution.py:1087
  36.4 18.8 %collective-permute-start.4 = (bf16[2,2,64,768]{3,2,1,0:T(8,128)(2,1)S(1)}, bf16[2,2,64,768]{3,2,1,0:T(8,128)(2,1)S(1)}, u32[]{:S(2)}, u32[]{:S(2)}) collective-permute-start(bf16[2,2,64,768]{3,2,1,0:T(8,128)(2,1)S(1)} %pad_maximum_fusion.4), channel_id=1, source_target_pairs={{0,8},{4,12},{8,0},{12,4},{16,24},{20,28},{24,16},{28,20},{1,9},{5... | collective-permute-start | bytes 1179656 | tf_op jit(solution)/shard_map/ppermute | solution.py:1087
  56.2 18.0 %collective-permute-start.7 = (bf16[4,2,64,768]{3,2,1,0:T(8,128)(2,1)}, bf16[4,2,64,768]{3,2,1,0:T(8,128)(2,1)}, u32[]{:S(2)}, u32[]{:S(2)}) collective-permute-start(bf16[4,2,64,768]{3,2,1,0:T(8,128)(2,1)} %pad_maximum_fusion.1), channel_id=1, source_target_pairs={{0,8},{4,12},{8,0},{12,4},{16,24},{20,28},{24,16},{28,20},{1,9},{5... | collective-permute-start | bytes 2359304 | tf_op jit(solution)/shard_map/ppermute | solution.py:1087
  57.2 17.0 %collective-permute-start.6 = (bf16[4,2,64,768]{3,2,1,0:T(8,128)(2,1)}, bf16[4,2,64,768]{3,2,1,0:T(8,128)(2,1)}, u32[]{:S(2)}, u32[]{:S(2)}) collective-permute-start(bf16[4,2,64,768]{3,2,1,0:T(8,128)(2,1)} %pad_maximum_fusion), channel_id=1, source_target_pairs={{0,4},{4,0},{8,12},{12,8},{16,20},{20,16},{24,28},{28,24},{1,5},{5... | collective-permute-start | bytes 2359304 | tf_op jit(solution)/shard_map/ppermute | solution.py:1087
  142.8 17.8 %collective-permute-start.8 = (bf16[2,2,2,72,768]{4,3,2,1,0:T(8,128)(2,1)S(1)}, bf16[2,2,2,72,768]{4,3,2,1,0:T(8,128)(2,1)S(1)}, u32[]{:S(2)}, u32[]{:S(2)}) collective-permute-start(bf16[2,2,2,72,768]{4,3,2,1,0:T(8,128)(2,1)S(1)} %bitcast.215), channel_id=1, source_target_pairs={{0,4},{4,0},{8,12},{12,8},{16,20},{20,16},{24,28},{28,24},{1,5},{5... | collective-permute-start | bytes 2654216 | tf_op jit(solution)/shard_map/ppermute | solution.py:1087
  144.4 18.0 %collective-permute-start.9 = (bf16[2,2,2,72,768]{4,3,2,1,0:T(8,128)(2,1)S(1)}, bf16[2,2,2,72,768]{4,3,2,1,0:T(8,128)(2,1)S(1)}, u32[]{:S(2)}, u32[]{:S(2)}) collective-permute-start(bf16[2,2,2,72,768]{4,3,2,1,0:T(8,128)(2,1)S(1)} %bitcast.214), channel_id=1, source_target_pairs={{0,8},{4,12},{8,0},{12,4},{16,24},{20,28},{24,16},{28,20},{1,9},{5... | collective-permute-start | bytes 2654216 | tf_op jit(solution)/shard_map/ppermute | solution.py:1087
  162.5 26.2 %collective-permute-start.11 = (bf16[2,2,72,768]{3,2,1,0:T(8,128)(2,1)S(1)}, bf16[2,2,72,768]{3,2,1,0:T(8,128)(2,1)S(1)}, u32[]{:S(2)}, u32[]{:S(2)}) collective-permute-start(bf16[2,2,72,768]{3,2,1,0:T(8,128)(2,1)S(1)} %get-tuple-element.267), channel_id=1, source_target_pairs={{0,16},{4,20},{8,24},{12,28},{16,0},{20,4},{24,8},{28,12},{1,17},{... | collective-permute-start | bytes 1327112 | tf_op jit(solution)/shard_map/ppermute | solution.py:1087
  168.5 20.1 %collective-permute-start.10 = (bf16[2,2,72,768]{3,2,1,0:T(8,128)(2,1)S(1)}, bf16[2,2,72,768]{3,2,1,0:T(8,128)(2,1)S(1)}, u32[]{:S(2)}, u32[]{:S(2)}) collective-permute-start(bf16[2,2,72,768]{3,2,1,0:T(8,128)(2,1)S(1)} %get-tuple-element.268), channel_id=1, source_target_pairs={{0,8},{4,12},{8,0},{12,4},{16,24},{20,28},{24,16},{28,20},{1,9},{5... | collective-permute-start | bytes 1327112 | tf_op jit(solution)/shard_map/ppermute | solution.py:1087
  189.6 20.1 %collective-permute-start.15 = (bf16[2,72,768]{2,1,0:T(8,128)(2,1)}, bf16[2,72,768]{2,1,0:T(8,128)(2,1)}, u32[]{:S(2)}, u32[]{:S(2)}) collective-permute-start(bf16[2,72,768]{2,1,0:T(8,128)(2,1)} %get-tuple-element.271), channel_id=1, source_target_pairs={{0,4},{4,0},{8,12},{12,8},{16,20},{20,16},{24,28},{28,24},{1,5},{5... | collective-permute-start | bytes 663560 | tf_op jit(solution)/shard_map/ppermute | solution.py:1087
  223.8 22.9 %collective-permute-start.17 = (bf16[2,2,2,208,384]{4,3,2,1,0:T(8,128)(2,1)}, bf16[2,2,2,208,384]{4,3,2,1,0:T(8,128)(2,1)}, u32[]{:S(2)}, u32[]{:S(2)}) collective-permute-start(bf16[2,2,2,208,384]{4,3,2,1,0:T(8,128)(2,1)} %get-tuple-element.226), channel_id=1, source_target_pairs={{0,1},{1,0},{2,3},{3,2},{4,5},{5,4},{6,7},{7,6},{8,9},{9,8},{10,11... | collective-permute-start | bytes 3833864 | tf_op jit(solution)/shard_map/ppermute | solution.py:1087
  225.3 21.4 %collective-permute-start.18 = (bf16[2,2,2,144,384]{4,3,2,1,0:T(8,128)(2,1)}, bf16[2,2,2,144,384]{4,3,2,1,0:T(8,128)(2,1)}, u32[]{:S(2)}, u32[]{:S(2)}) collective-permute-start(bf16[2,2,2,144,384]{4,3,2,1,0:T(8,128)(2,1)} %fusion), channel_id=1, source_target_pairs={{0,2},{1,3},{2,0},{3,1},{4,6},{5,7},{6,4},{7,5},{8,10},{9,11},{10,... | collective-permute-start | bytes 2654216 | tf_op jit(solution)/shard_map/ppermute | solution.py:1087
  229.0 17.7 %collective-permute-start.19 = (bf16[2,2,216,384]{3,2,1,0:T(8,128)(2,1)S(1)}, bf16[2,2,216,384]{3,2,1,0:T(8,128)(2,1)S(1)}, u32[]{:S(2)}, u32[]{:S(2)}) collective-permute-start(bf16[2,2,216,384]{3,2,1,0:T(8,128)(2,1)S(1)} %slice_bitcast_fusion.3), channel_id=1, source_target_pairs={{0,4},{4,0},{8,12},{12,8},{16,20},{20,16},{24,28},{28,24},{1,5},{5... | collective-permute-start | bytes 1990664 | tf_op jit(solution)/shard_map/ppermute | solution.py:1087
  230.1 16.6 %collective-permute-start.20 = (bf16[2,2,216,384]{3,2,1,0:T(8,128)(2,1)S(1)}, bf16[2,2,216,384]{3,2,1,0:T(8,128)(2,1)S(1)}, u32[]{:S(2)}, u32[]{:S(2)}) collective-permute-start(bf16[2,2,216,384]{3,2,1,0:T(8,128)(2,1)S(1)} %slice_bitcast_fusion.2), channel_id=1, source_target_pairs={{0,8},{4,12},{8,0},{12,4},{16,24},{20,28},{24,16},{28,20},{1,9},{5... | collective-permute-start | bytes 1990664 | tf_op jit(solution)/shard_map/ppermute | solution.py:1087
  248.1 22.1 %collective-permute-start.21 = (bf16[2,2,208,384]{3,2,1,0:T(8,128)(2,1)S(1)}, bf16[2,2,208,384]{3,2,1,0:T(8,128)(2,1)S(1)}, u32[]{:S(2)}, u32[]{:S(2)}) collective-permute-start(bf16[2,2,208,384]{3,2,1,0:T(8,128)(2,1)S(1)} %fusion.6), channel_id=1, source_target_pairs={{0,4},{4,0},{8,12},{12,8},{16,20},{20,16},{24,28},{28,24},{1,5},{5... | collective-permute-start | bytes 1916936 | tf_op jit(solution)/shard_map/ppermute | solution.py:1087
  250.1 20.2 %collective-permute-start.22 = (bf16[2,2,144,384]{3,2,1,0:T(8,128)(2,1)S(1)}, bf16[2,2,144,384]{3,2,1,0:T(8,128)(2,1)S(1)}, u32[]{:S(2)}, u32[]{:S(2)}) collective-permute-start(bf16[2,2,144,384]{3,2,1,0:T(8,128)(2,1)S(1)} %fusion.8), channel_id=1, source_target_pairs={{0,8},{4,12},{8,0},{12,4},{16,24},{20,28},{24,16},{28,20},{1,9},{5... | collective-permute-start | bytes 1327112 | tf_op jit(solution)/shard_map/ppermute | solution.py:1087
  251.0 16.4 %collective-permute-start.23 = (bf16[2,216,384]{2,1,0:T(8,128)(2,1)S(1)}, bf16[2,216,384]{2,1,0:T(8,128)(2,1)S(1)}, u32[]{:S(2)}, u32[]{:S(2)}) collective-permute-start(bf16[2,216,384]{2,1,0:T(8,128)(2,1)S(1)} %get-tuple-element.265), channel_id=1, source_target_pairs={{0,8},{4,12},{8,0},{12,4},{16,24},{20,28},{24,16},{28,20},{1,9},{5... | collective-permute-start | bytes 995336 | tf_op jit(solution)/shard_map/ppermute | solution.py:1087
  251.8 18.4 %collective-permute-start.24 = (bf16[2,216,384]{2,1,0:T(8,128)(2,1)S(1)}, bf16[2,216,384]{2,1,0:T(8,128)(2,1)S(1)}, u32[]{:S(2)}, u32[]{:S(2)}) collective-permute-start(bf16[2,216,384]{2,1,0:T(8,128)(2,1)S(1)} %get-tuple-element.264), channel_id=1, source_target_pairs={{0,4},{4,0},{8,12},{12,8},{16,20},{20,16},{24,28},{28,24},{1,5},{5... | collective-permute-start | bytes 995336 | tf_op jit(solution)/shard_map/ppermute | solution.py:1087
  270.5 17.6 %collective-permute-start.27 = (bf16[432,384]{1,0:T(8,128)(2,1)S(1)}, bf16[432,384]{1,0:T(8,128)(2,1)S(1)}, u32[]{:S(2)}, u32[]{:S(2)}) collective-permute-start(bf16[432,384]{1,0:T(8,128)(2,1)S(1)} %pad_maximum_fusion.6), channel_id=1, source_target_pairs={{0,16},{4,20},{8,24},{12,28},{16,0},{20,4},{24,8},{28,12},{1,17},{... | collective-permute-start | bytes 995336 | tf_op jit(solution)/shard_map/ppermute | solution.py:1087
  288.2 15.4 %collective-permute-start.30 = (bf16[432,384]{1,0:T(8,128)(2,1)S(1)}, bf16[432,384]{1,0:T(8,128)(2,1)S(1)}, u32[]{:S(2)}, u32[]{:S(2)}) collective-permute-start(bf16[432,384]{1,0:T(8,128)(2,1)S(1)} %fusion.3.low), channel_id=1, source_target_pairs={{0,2},{1,3},{2,0},{3,1},{4,6},{5,7},{6,4},{7,5},{8,10},{9,11},{10,... | collective-permute-start | bytes 995336 | tf_op jit(solution)/shard_map/ppermute | solution.py:1087
  290.2 13.4 %collective-permute-start.28 = (bf16[208,384]{1,0:T(8,128)(2,1)S(1)}, bf16[208,384]{1,0:T(8,128)(2,1)S(1)}, u32[]{:S(2)}, u32[]{:S(2)}) collective-permute-start(bf16[208,384]{1,0:T(8,128)(2,1)S(1)} %fusion.18), channel_id=1, source_target_pairs={{0,16},{4,20},{8,24},{12,28},{16,0},{20,4},{24,8},{28,12},{1,17},{... | collective-permute-start | bytes 479240 | tf_op jit(solution)/shard_map/ppermute | solution.py:1087
  291.3 12.3 %collective-permute-start.29 = (bf16[144,384]{1,0:T(8,128)(2,1)S(1)}, bf16[144,384]{1,0:T(8,128)(2,1)S(1)}, u32[]{:S(2)}, u32[]{:S(2)}) collective-permute-start(bf16[144,384]{1,0:T(8,128)(2,1)S(1)} %fusion.21), channel_id=1, source_target_pairs={{0,16},{4,20},{8,24},{12,28},{16,0},{20,4},{24,8},{28,12},{1,17},{... | collective-permute-start | bytes 331784 | tf_op jit(solution)/shard_map/ppermute | solution.py:1087
  (99 other events, 656.3 us)
Sparse Core Ops, SparseCore 0:
  127.9 89.8 reduce-scatter.1
where the time goes:
time: 334 us; the launch traced here: 329 us
  Pallas kernels  115 us (34%)
  waiting for transfers between devices  91.6 us (27%)
  starting transfers between devices  54.7 us (16%)
  local copies, waits for them, and re-layouts  36.9 us (11%)
  other arithmetic  15.7 us (5%)
  between operations  15.3 us (5%)
    pallas_call x18, Pallas kernels, call(): pl.pallas_call(body, grid_spec=pltpu.PrefetchScalarGridSpec(num_scalar_pr...  115 us
    ppermute x30, waiting for transfers between devices, swap(): return lax.ppermute(value, axis, [(i, i ^ 1 << bit) for i in range(count)])  84.2 us
    ppermute x30, starting transfers between devices, swap(): return lax.ppermute(value, axis, [(i, i ^ 1 << bit) for i in range(count)])  45.6 us
    unnamed x176, local copies, waits for them, and re-layouts  25.6 us
    ppermute x4, starting transfers between devices, shift(): return lax.ppermute(value, axis, pairs)  9.07 us
    ppermute x4, waiting for transfers between devices, shift(): return lax.ppermute(value, axis, pairs)  7.45 us
    convert_element_type x7, other arithmetic, advance(): came = swap(total_of(terms, 1).astype(BF16), *hop)  6.87 us
  transfers between devices with their start and end apart: 35, of which 15 were waited for; matrix products, arithmetic and copies ran while one was open for 6% of the time, Pallas kernels for 18%

commit v1 on v0

--- a/solution.py
+++ b/solution.py
@@ -1026,6 +1026,12 @@
     quarters[1 - odd, 1 - upper] = across[1]
 
 
+def order_parts(spots, parts, quarters):
+    odd, upper = spots[0], spots[1]
+    for flip, part in enumerate(parts):
+        quarters[odd ^ (flip & 1), upper ^ (flip >> 1)] = part[...]
+
+
 def join_square(quarters, start, out):
     for core in range(2):
         for side in range(2):
@@ -1059,9 +1065,9 @@
     )
 
 
-def collect_last_body(spots, low, other, across, *refs, cut):
-    pq, lo, lq, lk, lv, vectors, quarters = refs
-    order_quarters(spots, low, other, across, quarters)
+def collect_last_body(spots, *refs, cut):
+    pq, lo, lq, lk, lv, vectors, quarters = refs[4:]
+    order_parts(spots, refs[:4], quarters)
     for index, out in enumerate((pq, lo, lq)):
         join_square(quarters, index * 48, out)
     for core in range(2):
@@ -1071,14 +1077,14 @@
         vectors[core] = half[192:208]
 
 
-def collect_last(spots, low, other, across, cut):
+def collect_last(spots, parts, cut):
     return call(
         functools.partial(collect_last_body, cut=cut),
         (1,),
         (spots,),
-        [whole(low), whole(other), whole(across)],
+        [whole(part) for part in parts],
         [out_whole((96, 768), F32)] * 5 + [out_whole((2, 16, 384), F32)],
-        [pltpu.VMEM((2, 2) + low.shape, BF16)],
+        [pltpu.VMEM((2, 2) + parts[0].shape, BF16)],
     )
 
 
@@ -1297,16 +1303,13 @@
             came = [swap(sent[which], "seq", back[which][stage]) for which in range(2)]
             if stage < docs:
                 back_parts = list(back_step(stage, token))
-            if stage == docs - 1:
-                from_left = shift(back_parts[3], "seq", 1)
-                from_right = shift(back_parts[2], "seq", -1)
             if fast and stage == 0:
                 came[0], came[1], back_parts[0], token = sync(
                     came[0], came[1], back_parts[0], token
                 )
             if fast and stage == 1:
-                came[0], came[1], from_left, from_right, token = sync(
-                    came[0], came[1], from_left, from_right, token
+                came[0], came[1], back_parts[2], back_parts[3], token = sync(
+                    came[0], came[1], back_parts[2], back_parts[3], token
                 )
             if fast and stage == 2:
                 middle_kept, middle_sent = scatter_products(
@@ -1318,8 +1321,10 @@
                         ("square", tokens(inputs), tokens(back_parts[0])),
                     ],
                 )
-                came[0], came[1], middle_sent, token = sync(
-                    came[0], came[1], middle_sent, token
+                from_left = shift(back_parts[3], "seq", 1)
+                from_right = shift(back_parts[2], "seq", -1)
+                came[0], came[1], from_left, from_right, middle_sent, token = sync(
+                    came[0], came[1], from_left, from_right, middle_sent, token
                 )
             if stage < levels - 1:
                 for which in range(2):
@@ -1337,6 +1342,7 @@
             pooled_grads += [total, jnp.zeros_like(total)]
         for doc in range(docs):
             back_parts = back_step(doc, token)
+    if not fast:
         from_left = shift(back_parts[3], "seq", 1)
         from_right = shift(back_parts[2], "seq", -1)
     dq, own_grads = back_parts[:2]
@@ -1361,7 +1367,7 @@
     )
 
     if fast:
-        cut_feed = feed_part.shape[-2] // 2
+        cut_feed = 240
         one = [feed_part[..., :cut_feed, :]]
         two = [feed_part[..., cut_feed:, :]]
 
@@ -1404,14 +1410,19 @@
                 total_of(last_terms + [last_came], Ellipsis),
             ]
         ).astype(BF16)
-        other = swap(low, "batch", 1)
+        parts = [low] + [
+            lax.ppermute(low, "batch", [(each, each ^ flip) for each in range(4)])
+            for flip in range(1, 4)
+        ]
         feed_across = swap(jnp.stack([feed_low, feed_other]), "batch", 0)
-        low, other, feed_across = sync(low, other, feed_across)
-        across = swap(jnp.stack([low, other]), "batch", 0)
         spots = jnp.stack([mine & 1, mine >> 1]).astype(jnp.int32)
         grad_expand, grad_reduce, grad_po = collect_feed(spots, feed_low, feed_other, feed_across)
+        *others, grad_expand, grad_reduce, grad_po = sync(
+            *parts[1:], grad_expand, grad_reduce, grad_po
+        )
+        parts = parts[:1] + others
         grad_pq, grad_lo, grad_lq, grad_lk, grad_lv, lines = collect_last(
-            spots, low, other, across, cut_at
+            spots, parts, cut_at
         )
         vec_low, vec_high = lines[0, :, :96], lines[1, :, :96]
         (fg, fs, rb, ng, ns, pob) = [vec_low[index] for index in range(6)]

time: 334 us -> 332 us (level)
  waiting for transfers between devices: 91.6 us -> 100 us
  starting transfers between devices: 54.7 us -> 49.5 us
  other arithmetic: 15.7 us -> 11.6 us
    ppermute x0 -> x3, waiting for transfers between devices: none -> 9.44 us  [device_step(): lax.ppermute(low, 'batch', [(each, each ^ flip) for each in range(4)])]
    ppermute x30 -> x28, starting transfers between devices: 45.6 us -> 37.5 us  [swap(): return lax.ppermute(value, axis, [(i, i ^ 1 << bit) for i in range(count)])]
    convert_element_type x7 -> x8, other arithmetic: 6.87 us -> 3.74 us  [advance(): came = swap(total_of(terms, 1).astype(BF16), *hop)]
    ppermute x30 -> x28, waiting for transfers between devices: 84.2 us -> 86.4 us  [swap(): return lax.ppermute(value, axis, [(i, i ^ 1 << bit) for i in range(count)])]
    unnamed x176 -> x172, local copies, waits for them, and re-layouts: 25.6 us -> 24 us
  transfers between devices with their start and end apart: 35 -> 36, of which waited for: 15 -> 15; matrix products, arithmetic and copies ran while one was open for 6% -> 6% of each run, Pallas kernels for 18% -> 18%
where the time goes in v1:
time: 332 us; the launch traced here: 327 us
  Pallas kernels  115 us (35%)
  waiting for transfers between devices  100 us (30%)
  starting transfers between devices  49.5 us (15%)
  local copies, waits for them, and re-layouts  35.2 us (11%)
  between operations  15.3 us (5%)
  other arithmetic  11.6 us (3%)
    pallas_call x18, Pallas kernels, call(): pl.pallas_call(body, grid_spec=pltpu.PrefetchScalarGridSpec(num_scalar_pr...  115 us
    ppermute x28, waiting for transfers between devices, swap(): return lax.ppermute(value, axis, [(i, i ^ 1 << bit) for i in range(count)])  86.4 us
    ppermute x28, starting transfers between devices, swap(): return lax.ppermute(value, axis, [(i, i ^ 1 << bit) for i in range(count)])  37.5 us
    unnamed x172, local copies, waits for them, and re-layouts  24 us
    ppermute x4, starting transfers between devices, shift(): return lax.ppermute(value, axis, pairs)  9.81 us
    ppermute x3, waiting for transfers between devices, device_step(): lax.ppermute(low, 'batch', [(each, each ^ flip) for each in range(4)])  9.44 us
  transfers between devices with their start and end apart: 36, of which 15 were waited for; matrix products, arithmetic and copies ran while one was open for 6% of the time, Pallas kernels for 18%

profile of v1, /device:TPU:1, one launch (start us, length us, event | category | flops | bytes accessed | tf_op | source)
XLA Modules:
  0.0 327.2 jit_solution(17677359049130953719)
XLA Ops:
  15.7 4.8 %shard_map.460 = (bf16[2,256,768]{2,1,0:T(8,128)(2,1)S(1)}, bf16[2,256,768]{2,1,0:T(8,128)(2,1)S(1)}, bf16[2,256,768]{2,1,0:T(8,128)(2,1)S(1)}, bf16[768,768]{1,0:T(8,128)(2,1)S(1)}, bf16[768,768]{1,0:T(8,128)(2,1)S(1)}) custom-call(s32[4]{0:T(128)S(1)} %pad_add_fusion.1.place.token, bf16[2,256,768]{2,1,0:T(8,128)(2,1)} %x.1, bf16[768,768]{1,0:T(8,128)(2,1)} %wq.1, ...), custom_call_target="tpu_custom_call" | custom-call | flops 1000 | bytes 1000 | tf_op jit(solution)/shard_map/pallas_call | solution.py:72
  22.6 4.7 %collective-permute-start.2 = (bf16[1,2,64,768]{3,2,1,0:T(8,128)(2,1)S(1)}, bf16[1,2,64,768]{3,2,1,0:T(8,128)(2,1)S(1)}, u32[]{:S(2)}, u32[]{:S(2)}) collective-permute-start(bf16[1,2,64,768]{3,2,1,0:T(8,128)(2,1)S(1)} %get-tuple-element.283.refs_0_), channel_id=1, source_target_pairs={{0,16},{4,20},{8,24},{12,28},{16,0},{20,4},{24,8},{28,12},{1,17},{... | collective-permute-start | bytes 589832 | tf_op jit(solution)/shard_map/ppermute | solution.py:1093
  27.3 8.9 %collective-permute-done.2.refs_1_ = bf16[1,2,64,768]{3,2,1,0:T(8,128)(2,1)S(1)} collective-permute-done((bf16[1,2,64,768]{3,2,1,0:T(8,128)(2,1)S(1)}, bf16[1,2,64,768]{3,2,1,0:T(8,128)(2,1)S(1)}, u32[]{:S(2)}, u32[]{:S(2)}) %collective-permute-start.2) | collective-permute-done | bytes 196640 | tf_op jit(solution)/shard_map/ppermute | solution.py:1093
  36.4 4.3 %collective-permute-start.4 = (bf16[2,2,64,768]{3,2,1,0:T(8,128)(2,1)S(1)}, bf16[2,2,64,768]{3,2,1,0:T(8,128)(2,1)S(1)}, u32[]{:S(2)}, u32[]{:S(2)}) collective-permute-start(bf16[2,2,64,768]{3,2,1,0:T(8,128)(2,1)S(1)} %pad_maximum_fusion.3), channel_id=1, source_target_pairs={{0,8},{4,12},{8,0},{12,4},{16,24},{20,28},{24,16},{28,20},{1,9},{5... | collective-permute-start | bytes 1179656 | tf_op jit(solution)/shard_map/ppermute | solution.py:1093
  40.6 4.8 %shard_map.462 = (bf16[256,768]{1,0:T(8,128)(2,1)S(1)}, f32[6,2,256,256]{3,2,1,0:T(8,128)S(1)}) custom-call(s32[4]{0:T(128)S(1)} %pad_add_fusion.1.place.token, bf16[2,256,768]{2,1,0:T(8,128)(2,1)S(1)} %get-tuple-element.157.q, bf16[2,384,768]{2,1,0:T(8,128)(2,1)S(1)} %get-tuple-element.158.kx.refs_4_, bf16[2,384,768]{2,1,0:T(8,128)(2,1)S(1)} %get-tuple-element.159.vx.refs_5_), custom_call_target="tpu_custom_call" | custom-call | flops 1000 | bytes 1000 | tf_op jit(solution)/shard_map/pallas_call | solution.py:72
  47.9 7.3 %collective-permute-done.5.refs_6_ = bf16[2,2,64,768]{3,2,1,0:T(8,128)(2,1)S(1)} collective-permute-done((bf16[2,2,64,768]{3,2,1,0:T(8,128)(2,1)S(1)}, bf16[2,2,64,768]{3,2,1,0:T(8,128)(2,1)S(1)}, u32[]{:S(2)}, u32[]{:S(2)}) %collective-permute-start.5) | collective-permute-done | bytes 393248 | tf_op jit(solution)/shard_map/ppermute | solution.py:1093
  61.4 4.8 %shard_map.463 = (bf16[256,768]{1,0:T(8,128)(2,1)S(1)}, f32[6,2,256,256]{3,2,1,0:T(8,128)S(1)}) custom-call(s32[4]{0:T(128)S(1)} %pad_add_fusion.1.place.token, bf16[2,256,768]{2,1,0:T(8,128)(2,1)S(1)} %copy-done.2, bf16[2,384,768]{2,1,0:T(8,128)(2,1)S(1)} %get-tuple-element.158.kx.refs_4_, bf16[2,384,768]{2,1,0:T(8,128)(2,1)S(1)} %get-tuple-element.159.vx.refs_5_), custom_call_target="tpu_custom_call" | custom-call | flops 1000 | bytes 1000 | tf_op jit(solution)/shard_map/pallas_call | solution.py:72
  74.4 24.3 %shard_map.465 = (bf16[2,512,768]{2,1,0:T(8,128)(2,1)}, bf16[2,512,768]{2,1,0:T(8,128)(2,1)}, f32[2,6,512,512]{3,2,1,0:T(8,128)}, bf16[2,256,768]{2,1,0:T(8,128)...) custom-call(s32[4]{0:T(128)S(1)} %pad_add_fusion.1.place.token, ...), custom_call_target="tpu_custom_call" | custom-call | flops 1000 | bytes 1000 | tf_op jit(solution)/shard_map/pallas_call | solution.py:72
  98.7 18.2 %shard_map.466 = (bf16[2,256,768]{2,1,0:T(8,128)(2,1)}, bf16[512,768]{1,0:T(8,128)(2,1)S(1)}, bf16[512,3072]{1,0:T(8,128)(2,1)S(1)}, bf16[512,768]{1,0:T(8,128)(...) custom-call(s32[4]{0:T(128)S(1)} %pad_add_fusion.1.place.token, ...), custom_call_target="tpu_custom_call" | custom-call | flops 1000 | bytes 1000 | tf_op jit(solution)/shard_map/pallas_call | solution.py:72
  116.9 10.4 %shard_map.467 = bf16[2,2,2,2,2,432,384]{6,5,4,3,2,1,0:T(8,128)(2,1)} custom-call(s32[3]{0:T(128)S(1)} %pad_add_fusion.3.bits, bf16[512,768]{1,0:T(8,128)(2,1)S(1)} %get-tuple-element.176.refs_0_, bf16[512,3072]{1,0:T(8,128)(2,1)S(1)} %get-tuple-element.177.refs_1_, bf16[512,768]{1,0:T(8,128)(2,1)S(1)} %get-tuple-element.178.refs_2_, ...), custom_call_target="tpu_custom_call" | custom-call | flops 1000 | bytes 1000 | tf_op jit(solution)/shard_map/pallas_call | solution.py:72
  128.1 14.3 %shard_map.468 = (bf16[2,256,768]{2,1,0:T(8,128)(2,1)S(1)}, f32[4,2,72,768]{3,2,1,0:T(8,128)S(1)}, bf16[4,2,72,768]{3,2,1,0:T(8,128)(2,1)S(1)}, f32[4,2,72,768]{3,2,1,0:T(8,128)S(1)}, bf16[4,2,72,768]{3,2,1,0:T(8,128)(2,1)S(1)}) custom-call(s32[2,8]{1,0:T(2,128)S(1)} %copy-done.71, s32[4]{0:T(128)S(1)} %pad_add_fusion.1.place.token, ...), custom_call_target="tpu_custom_call" | custom-call | flops 1000 | bytes 1000 | tf_op jit(solution)/shard_map/pallas_call | solution.py:72
  148.5 4.5 %shard_map.470 = (bf16[1,256,768]{2,1,0:T(8,128)(2,1)S(1)}, f32[1,2,256,768]{3,2,1,0:T(8,128)S(1)}, bf16[1,2,64,768]{3,2,1,0:T(8,128)(2,1)S(1)}, bf16[1,2,64,768]{3,2,1,0:T(8,128)(2,1)S(1)}) custom-call(s32[4]{0:T(128)S(1)} %pad_add_fusion.1.place.token, bf16[2,256,768]{2,1,0:T(8,128)(2,1)S(1)} %copy-done.3, ...), custom_call_target="tpu_custom_call" | custom-call | flops 1000 | bytes 1000 | tf_op jit(solution)/shard_map/pallas_call | solution.py:72
  153.0 7.3 %collective-permute-done.8 = bf16[2,2,2,72,768]{4,3,2,1,0:T(8,128)(2,1)S(1)} collective-permute-done((bf16[2,2,2,72,768]{4,3,2,1,0:T(8,128)(2,1)S(1)}, bf16[2,2,2,72,768]{4,3,2,1,0:T(8,128)(2,1)S(1)}, u32[]{:S(2)}, u32[]{:S(2)}) %collective-permute-start.8) | collective-permute-done | bytes 884768 | tf_op jit(solution)/shard_map/ppermute | solution.py:1093
  162.1 5.8 %collective-permute-start.11 = (bf16[2,2,72,768]{3,2,1,0:T(8,128)(2,1)S(1)}, bf16[2,2,72,768]{3,2,1,0:T(8,128)(2,1)S(1)}, u32[]{:S(2)}, u32[]{:S(2)}) collective-permute-start(bf16[2,2,72,768]{3,2,1,0:T(8,128)(2,1)S(1)} %get-tuple-element.273), channel_id=1, source_target_pairs={{0,16},{4,20},{8,24},{12,28},{16,0},{20,4},{24,8},{28,12},{1,17},{... | collective-permute-start | bytes 1327112 | tf_op jit(solution)/shard_map/ppermute | solution.py:1093
  169.8 5.4 %shard_map.471 = (bf16[2,256,768]{2,1,0:T(8,128)(2,1)S(1)}, f32[2,2,256,768]{3,2,1,0:T(8,128)S(1)}, bf16[2,2,64,768]{3,2,1,0:T(8,128)(2,1)}, bf16[2,2,64,768]{3,2,1,0:T(8,128)(2,1)}) custom-call(s32[4]{0:T(128)S(1)} %pad_add_fusion.1.place.token, bf16[2,256,768]{2,1,0:T(8,128)(2,1)S(1)} %copy-done.3, bf16[2,384,768]{2,1,0:T(8,128)(2,1)S(1)} %get-tuple-element.158.kx.refs_4_, ...), custom_call_target="tpu_custom_call" | custom-call | flops 1000 | bytes 1000 | tf_op jit(solution)/shard_map/pallas_call | solution.py:72
  176.9 9.9 %collective-permute-done.11 = bf16[2,2,72,768]{3,2,1,0:T(8,128)(2,1)S(1)} collective-permute-done((bf16[2,2,72,768]{3,2,1,0:T(8,128)(2,1)S(1)}, bf16[2,2,72,768]{3,2,1,0:T(8,128)(2,1)S(1)}, u32[]{:S(2)}, u32[]{:S(2)}) %collective-permute-start.11) | collective-permute-done | bytes 442400 | tf_op jit(solution)/shard_map/ppermute | solution.py:1093
  204.6 4.1 %collective-permute-done.14.refs_9_ = bf16[2,2,64,768]{3,2,1,0:T(8,128)(2,1)S(1)} collective-permute-done((bf16[2,2,64,768]{3,2,1,0:T(8,128)(2,1)}, bf16[2,2,64,768]{3,2,1,0:T(8,128)(2,1)S(1)}, u32[]{:S(2)}, u32[]{:S(2)}) %collective-permute-start.14) | collective-permute-done | bytes 393248 | tf_op jit(solution)/shard_map/ppermute | solution.py:1099
  208.7 5.4 %collective-permute-start.16 = (bf16[2,2,2,2,144,384]{5,4,3,2,1,0:T(8,128)(2,1)S(1)}, bf16[2,2,2,2,144,384]{5,4,3,2,1,0:T(8,128)(2,1)S(1)}, u32[]{:S(2)}, u32[]{:S(2)}) collective-permute-start(bf16[2,2,2,2,144,384]{5,4,3,2,1,0:T(8,128)(2,1)S(1)} %get-tuple-element.230), channel_id=1, source_target_pairs={{0,1},{1,0},{2,3},{3,2},{4,5},{5,4},{6,7},{7,6},{8,9},{9,8},{10,11... | collective-permute-start | bytes 5308424 | tf_op jit(solution)/shard_map/ppermute | solution.py:1093
  235.5 11.1 %collective-permute-done.18 = bf16[2,2,2,144,384]{4,3,2,1,0:T(8,128)(2,1)} collective-permute-done((bf16[2,2,2,144,384]{4,3,2,1,0:T(8,128)(2,1)}, bf16[2,2,2,144,384]{4,3,2,1,0:T(8,128)(2,1)}, u32[]{:S(2)}, u32[]{:S(2)}) %collective-permute-start.18) | collective-permute-done | bytes 884768 | tf_op jit(solution)/shard_map/ppermute | solution.py:1093
  251.3 16.8 %collective-permute-done.24 = bf16[2,192,384]{2,1,0:T(8,128)(2,1)S(1)} collective-permute-done((bf16[2,192,384]{2,1,0:T(8,128)(2,1)S(1)}, bf16[2,192,384]{2,1,0:T(8,128)(2,1)S(1)}, u32[]{:S(2)}, u32[]{:S(2)}) %collective-permute-start.24) | collective-permute-done | bytes 294944 | tf_op jit(solution)/shard_map/ppermute | solution.py:1093
  271.4 4.9 %collective-permute-done.26 = bf16[2,144,384]{2,1,0:T(8,128)(2,1)S(1)} collective-permute-done((bf16[2,144,384]{2,1,0:T(8,128)(2,1)S(1)}, bf16[2,144,384]{2,1,0:T(8,128)(2,1)S(1)}, u32[]{:S(2)}, u32[]{:S(2)}) %collective-permute-start.26) | collective-permute-done | bytes 221216 | tf_op jit(solution)/shard_map/ppermute | solution.py:1093
  276.3 5.1 %collective-permute-done.25 = bf16[2,208,384]{2,1,0:T(8,128)(2,1)S(1)} collective-permute-done((bf16[2,208,384]{2,1,0:T(8,128)(2,1)S(1)}, bf16[2,208,384]{2,1,0:T(8,128)(2,1)S(1)}, u32[]{:S(2)}, u32[]{:S(2)}) %collective-permute-start.25) | collective-permute-done | bytes 319520 | tf_op jit(solution)/shard_map/ppermute | solution.py:1093
  290.1 9.2 %collective-permute-done.29 = bf16[144,384]{1,0:T(8,128)(2,1)S(1)} collective-permute-done((bf16[144,384]{1,0:T(8,128)(2,1)S(1)}, bf16[144,384]{1,0:T(8,128)(2,1)S(1)}, u32[]{:S(2)}, u32[]{:S(2)}) %collective-permute-start.29) | collective-permute-done | bytes 110624 | tf_op jit(solution)/shard_map/ppermute | solution.py:1093
  310.2 6.4 %collective-permute-done.33.refs_3_ = bf16[352,384]{1,0:T(8,128)(2,1)S(1)} collective-permute-done((bf16[352,384]{1,0:T(8,128)(2,1)S(1)}, bf16[352,384]{1,0:T(8,128)(2,1)S(1)}, u32[]{:S(2)}, u32[]{:S(2)}) %collective-permute-start.33) | collective-permute-done | bytes 270368 | tf_op jit(solution)/shard_map/ppermute | solution.py:1414
  (292 shorter events, 109.2 us)
Async XLA Ops:
  7.2 219.2 %reduce-scatter.2.cloned.1.call-start = ((), (), s32[]{:S(2)}) async-start(), calls=%async_computation.1 | async-start | bytes 13271040 | tf_op jit(solution)/shard_map/reduce_scatter | solution.py:1252
  36.2 18.9 %collective-permute-start.5 = (bf16[2,2,64,768]{3,2,1,0:T(8,128)(2,1)S(1)}, bf16[2,2,64,768]{3,2,1,0:T(8,128)(2,1)S(1)}, u32[]{:S(2)}, u32[]{:S(2)}) collective-permute-start(bf16[2,2,64,768]{3,2,1,0:T(8,128)(2,1)S(1)} %pad_maximum_fusion.4), channel_id=1, source_target_pairs={{0,16},{4,20},{8,24},{12,28},{16,0},{20,4},{24,8},{28,12},{1,17},{... | collective-permute-start | bytes 1179656 | tf_op jit(solution)/shard_map/ppermute | solution.py:1093
  36.4 18.8 %collective-permute-start.4 = (bf16[2,2,64,768]{3,2,1,0:T(8,128)(2,1)S(1)}, bf16[2,2,64,768]{3,2,1,0:T(8,128)(2,1)S(1)}, u32[]{:S(2)}, u32[]{:S(2)}) collective-permute-start(bf16[2,2,64,768]{3,2,1,0:T(8,128)(2,1)S(1)} %pad_maximum_fusion.3), channel_id=1, source_target_pairs={{0,8},{4,12},{8,0},{12,4},{16,24},{20,28},{24,16},{28,20},{1,9},{5... | collective-permute-start | bytes 1179656 | tf_op jit(solution)/shard_map/ppermute | solution.py:1093
  56.2 18.0 %collective-permute-start.7 = (bf16[4,2,64,768]{3,2,1,0:T(8,128)(2,1)}, bf16[4,2,64,768]{3,2,1,0:T(8,128)(2,1)}, u32[]{:S(2)}, u32[]{:S(2)}) collective-permute-start(bf16[4,2,64,768]{3,2,1,0:T(8,128)(2,1)} %pad_maximum_fusion.1), channel_id=1, source_target_pairs={{0,8},{4,12},{8,0},{12,4},{16,24},{20,28},{24,16},{28,20},{1,9},{5... | collective-permute-start | bytes 2359304 | tf_op jit(solution)/shard_map/ppermute | solution.py:1093
  57.2 17.1 %collective-permute-start.6 = (bf16[4,2,64,768]{3,2,1,0:T(8,128)(2,1)}, bf16[4,2,64,768]{3,2,1,0:T(8,128)(2,1)}, u32[]{:S(2)}, u32[]{:S(2)}) collective-permute-start(bf16[4,2,64,768]{3,2,1,0:T(8,128)(2,1)} %pad_maximum_fusion), channel_id=1, source_target_pairs={{0,4},{4,0},{8,12},{12,8},{16,20},{20,16},{24,28},{28,24},{1,5},{5... | collective-permute-start | bytes 2359304 | tf_op jit(solution)/shard_map/ppermute | solution.py:1093
  142.4 17.9 %collective-permute-start.8 = (bf16[2,2,2,72,768]{4,3,2,1,0:T(8,128)(2,1)S(1)}, bf16[2,2,2,72,768]{4,3,2,1,0:T(8,128)(2,1)S(1)}, u32[]{:S(2)}, u32[]{:S(2)}) collective-permute-start(bf16[2,2,2,72,768]{4,3,2,1,0:T(8,128)(2,1)S(1)} %bitcast.209), channel_id=1, source_target_pairs={{0,4},{4,0},{8,12},{12,8},{16,20},{20,16},{24,28},{28,24},{1,5},{5... | collective-permute-start | bytes 2654216 | tf_op jit(solution)/shard_map/ppermute | solution.py:1093
  143.9 18.0 %collective-permute-start.9 = (bf16[2,2,2,72,768]{4,3,2,1,0:T(8,128)(2,1)S(1)}, bf16[2,2,2,72,768]{4,3,2,1,0:T(8,128)(2,1)S(1)}, u32[]{:S(2)}, u32[]{:S(2)}) collective-permute-start(bf16[2,2,2,72,768]{4,3,2,1,0:T(8,128)(2,1)S(1)} %bitcast.208), channel_id=1, source_target_pairs={{0,8},{4,12},{8,0},{12,4},{16,24},{20,28},{24,16},{28,20},{1,9},{5... | collective-permute-start | bytes 2654216 | tf_op jit(solution)/shard_map/ppermute | solution.py:1093
  162.1 24.8 %collective-permute-start.11 = (bf16[2,2,72,768]{3,2,1,0:T(8,128)(2,1)S(1)}, bf16[2,2,72,768]{3,2,1,0:T(8,128)(2,1)S(1)}, u32[]{:S(2)}, u32[]{:S(2)}) collective-permute-start(bf16[2,2,72,768]{3,2,1,0:T(8,128)(2,1)S(1)} %get-tuple-element.273), channel_id=1, source_target_pairs={{0,16},{4,20},{8,24},{12,28},{16,0},{20,4},{24,8},{28,12},{1,17},{... | collective-permute-start | bytes 1327112 | tf_op jit(solution)/shard_map/ppermute | solution.py:1093
  168.0 18.8 %collective-permute-start.10 = (bf16[2,2,72,768]{3,2,1,0:T(8,128)(2,1)S(1)}, bf16[2,2,72,768]{3,2,1,0:T(8,128)(2,1)S(1)}, u32[]{:S(2)}, u32[]{:S(2)}) collective-permute-start(bf16[2,2,72,768]{3,2,1,0:T(8,128)(2,1)S(1)} %get-tuple-element.274), channel_id=1, source_target_pairs={{0,8},{4,12},{8,0},{12,4},{16,24},{20,28},{24,16},{28,20},{1,9},{5... | collective-permute-start | bytes 1327112 | tf_op jit(solution)/shard_map/ppermute | solution.py:1093
  187.8 16.3 %collective-permute-start.13 = (bf16[2,72,768]{2,1,0:T(8,128)(2,1)}, bf16[2,72,768]{2,1,0:T(8,128)(2,1)}, u32[]{:S(2)}, u32[]{:S(2)}) collective-permute-start(bf16[2,72,768]{2,1,0:T(8,128)(2,1)} %get-tuple-element.277), channel_id=1, source_target_pairs={{0,4},{4,0},{8,12},{12,8},{16,20},{20,16},{24,28},{28,24},{1,5},{5... | collective-permute-start | bytes 663560 | tf_op jit(solution)/shard_map/ppermute | solution.py:1093
  188.1 20.6 %collective-permute-start.14 = (bf16[2,2,64,768]{3,2,1,0:T(8,128)(2,1)}, bf16[2,2,64,768]{3,2,1,0:T(8,128)(2,1)S(1)}, u32[]{:S(2)}, u32[]{:S(2)}) collective-permute-start(bf16[2,2,64,768]{3,2,1,0:T(8,128)(2,1)} %get-tuple-element.209), channel_id=1, source_target_pairs={{0,4},{4,8},{8,12},{12,16},{16,20},{20,24},{24,28},{1,5},{5,9},{9,... | collective-permute-start | bytes 1179656 | tf_op jit(solution)/shard_map/ppermute | solution.py:1099
  191.2 17.5 %collective-permute-start.15 = (bf16[2,2,64,768]{3,2,1,0:T(8,128)(2,1)}, bf16[2,2,64,768]{3,2,1,0:T(8,128)(2,1)}, u32[]{:S(2)}, u32[]{:S(2)}) collective-permute-start(bf16[2,2,64,768]{3,2,1,0:T(8,128)(2,1)} %get-tuple-element.210), channel_id=1, source_target_pairs={{4,0},{8,4},{12,8},{16,12},{20,16},{24,20},{28,24},{5,1},{9,5},{13... | collective-permute-start | bytes 1179656 | tf_op jit(solution)/shard_map/ppermute | solution.py:1099
  208.7 15.0 %collective-permute-start.16 = (bf16[2,2,2,2,144,384]{5,4,3,2,1,0:T(8,128)(2,1)S(1)}, bf16[2,2,2,2,144,384]{5,4,3,2,1,0:T(8,128)(2,1)S(1)}, u32[]{:S(2)}, u32[]{:S(2)}) collective-permute-start(bf16[2,2,2,2,144,384]{5,4,3,2,1,0:T(8,128)(2,1)S(1)} %get-tuple-element.230), channel_id=1, source_target_pairs={{0,1},{1,0},{2,3},{3,2},{4,5},{5,4},{6,7},{7,6},{8,9},{9,8},{10,11... | collective-permute-start | bytes 5308424 | tf_op jit(solution)/shard_map/ppermute | solution.py:1093
  223.7 22.9 %collective-permute-start.17 = (bf16[2,2,2,208,384]{4,3,2,1,0:T(8,128)(2,1)}, bf16[2,2,2,208,384]{4,3,2,1,0:T(8,128)(2,1)S(1)}, u32[]{:S(2)}, u32[]{:S(2)}) collective-permute-start(bf16[2,2,2,208,384]{4,3,2,1,0:T(8,128)(2,1)} %get-tuple-element.233), channel_id=1, source_target_pairs={{0,1},{1,0},{2,3},{3,2},{4,5},{5,4},{6,7},{7,6},{8,9},{9,8},{10,11... | collective-permute-start | bytes 3833864 | tf_op jit(solution)/shard_map/ppermute | solution.py:1093
  225.2 21.4 %collective-permute-start.18 = (bf16[2,2,2,144,384]{4,3,2,1,0:T(8,128)(2,1)}, bf16[2,2,2,144,384]{4,3,2,1,0:T(8,128)(2,1)}, u32[]{:S(2)}, u32[]{:S(2)}) collective-permute-start(bf16[2,2,2,144,384]{4,3,2,1,0:T(8,128)(2,1)} %fusion), channel_id=1, source_target_pairs={{0,2},{1,3},{2,0},{3,1},{4,6},{5,7},{6,4},{7,5},{8,10},{9,11},{10,... | collective-permute-start | bytes 2654216 | tf_op jit(solution)/shard_map/ppermute | solution.py:1093
  227.8 18.8 %collective-permute-start.19 = (bf16[2,2,240,384]{3,2,1,0:T(8,128)(2,1)S(1)}, bf16[2,2,240,384]{3,2,1,0:T(8,128)(2,1)S(1)}, u32[]{:S(2)}, u32[]{:S(2)}) collective-permute-start(bf16[2,2,240,384]{3,2,1,0:T(8,128)(2,1)S(1)} %slice_bitcast_fusion.2), channel_id=1, source_target_pairs={{0,4},{4,0},{8,12},{12,8},{16,20},{20,16},{24,28},{28,24},{1,5},{5... | collective-permute-start | bytes 2211848 | tf_op jit(solution)/shard_map/ppermute | solution.py:1093
  229.1 17.5 %collective-permute-start.20 = (bf16[2,2,192,384]{3,2,1,0:T(8,128)(2,1)S(1)}, bf16[2,2,192,384]{3,2,1,0:T(8,128)(2,1)S(1)}, u32[]{:S(2)}, u32[]{:S(2)}) collective-permute-start(bf16[2,2,192,384]{3,2,1,0:T(8,128)(2,1)S(1)} %slice_bitcast_fusion.3), channel_id=1, source_target_pairs={{0,8},{4,12},{8,0},{12,4},{16,24},{20,28},{24,16},{28,20},{1,9},{5... | collective-permute-start | bytes 1769480 | tf_op jit(solution)/shard_map/ppermute | solution.py:1093
  246.7 21.4 %collective-permute-start.23 = (bf16[2,240,384]{2,1,0:T(8,128)(2,1)S(1)}, bf16[2,240,384]{2,1,0:T(8,128)(2,1)S(1)}, u32[]{:S(2)}, u32[]{:S(2)}) collective-permute-start(bf16[2,240,384]{2,1,0:T(8,128)(2,1)S(1)} %fusion.3), channel_id=1, source_target_pairs={{0,8},{4,12},{8,0},{12,4},{16,24},{20,28},{24,16},{28,20},{1,9},{5... | collective-permute-start | bytes 1105928 | tf_op jit(solution)/shard_map/ppermute | solution.py:1093
  247.0 21.2 %collective-permute-start.21 = (bf16[2,2,208,384]{3,2,1,0:T(8,128)(2,1)S(1)}, bf16[2,2,208,384]{3,2,1,0:T(8,128)(2,1)S(1)}, u32[]{:S(2)}, u32[]{:S(2)}) collective-permute-start(bf16[2,2,208,384]{3,2,1,0:T(8,128)(2,1)S(1)} %fusion.5), channel_id=1, source_target_pairs={{0,4},{4,0},{8,12},{12,8},{16,20},{20,16},{24,28},{28,24},{1,5},{5... | collective-permute-start | bytes 1916936 | tf_op jit(solution)/shard_map/ppermute | solution.py:1093
  248.2 19.9 %collective-permute-start.22 = (bf16[2,2,144,384]{3,2,1,0:T(8,128)(2,1)S(1)}, bf16[2,2,144,384]{3,2,1,0:T(8,128)(2,1)S(1)}, u32[]{:S(2)}, u32[]{:S(2)}) collective-permute-start(bf16[2,2,144,384]{3,2,1,0:T(8,128)(2,1)S(1)} %fusion.8), channel_id=1, source_target_pairs={{0,8},{4,12},{8,0},{12,4},{16,24},{20,28},{24,16},{28,20},{1,9},{5... | collective-permute-start | bytes 1327112 | tf_op jit(solution)/shard_map/ppermute | solution.py:1093
  249.8 18.3 %collective-permute-start.24 = (bf16[2,192,384]{2,1,0:T(8,128)(2,1)S(1)}, bf16[2,192,384]{2,1,0:T(8,128)(2,1)S(1)}, u32[]{:S(2)}, u32[]{:S(2)}) collective-permute-start(bf16[2,192,384]{2,1,0:T(8,128)(2,1)S(1)} %fusion.7), channel_id=1, source_target_pairs={{0,4},{4,0},{8,12},{12,8},{16,20},{20,16},{24,28},{28,24},{1,5},{5... | collective-permute-start | bytes 884744 | tf_op jit(solution)/shard_map/ppermute | solution.py:1093
  268.4 16.8 %collective-permute-start.27 = (bf16[432,384]{1,0:T(8,128)(2,1)S(1)}, bf16[432,384]{1,0:T(8,128)(2,1)S(1)}, u32[]{:S(2)}, u32[]{:S(2)}) collective-permute-start(bf16[432,384]{1,0:T(8,128)(2,1)S(1)} %pad_maximum_fusion.5), channel_id=1, source_target_pairs={{0,16},{4,20},{8,24},{12,28},{16,0},{20,4},{24,8},{28,12},{1,17},{... | collective-permute-start | bytes 995336 | tf_op jit(solution)/shard_map/ppermute | solution.py:1093
  285.3 14.0 %collective-permute-start.30 = (bf16[432,384]{1,0:T(8,128)(2,1)S(1)}, bf16[432,384]{1,0:T(8,128)(2,1)S(1)}, u32[]{:S(2)}, u32[]{:S(2)}) collective-permute-start(bf16[432,384]{1,0:T(8,128)(2,1)S(1)} %fusion.4.low), channel_id=1, source_target_pairs={{0,2},{1,3},{2,0},{3,1},{4,6},{5,7},{6,4},{7,5},{8,10},{9,11},{10,... | collective-permute-start | bytes 995336 | tf_op jit(solution)/shard_map/ppermute | solution.py:1093
  302.9 13.7 %collective-permute-start.33 = (bf16[352,384]{1,0:T(8,128)(2,1)S(1)}, bf16[352,384]{1,0:T(8,128)(2,1)S(1)}, u32[]{:S(2)}, u32[]{:S(2)}) collective-permute-start(bf16[352,384]{1,0:T(8,128)(2,1)S(1)} %pad_maximum_fusion.6.refs_0_), channel_id=1, source_target_pairs={{0,3},{1,2},{2,1},{3,0},{4,7},{5,6},{6,5},{7,4},{8,11},{9,10},{10,... | collective-permute-start | bytes 811016 | tf_op jit(solution)/shard_map/ppermute | solution.py:1414
  (98 other events, 707.4 us)
Sparse Core Ops, SparseCore 0:
  127.5 89.7 reduce-scatter.1
